TPU v7x, 128 devices: a whole 4x4x4 slice. The times are simulated.
128 devices in a mesh: ctx: 32 (over z, x, core), head: 4 (over y).
Axes of the slice: x: 4, y: 4, z: 4, core: 2. Of those that a mesh axis runs over, the one named last changes fastest.
Arguments:
- tokens: bfloat16 [16384, 4096], P('ctx', 'head'), may hold values from -6 to 6
- pair_weight: bfloat16 [4096, 256], replicated, may hold values from -0.09375 to 0.09375
- value_weight: bfloat16 [4096, 4096], P(None, 'head'), may hold values from -0.09375 to 0.09375
- output_weight: bfloat16 [4096, 4096], P('head'), may hold values from -0.09375 to 0.09375
- level_index: int32 [16384, 8], P('ctx'), may hold values from 0 to 15
- level_table: float32 [8, 16, 32], P(None, None, 'head'), may hold values from 0.05 to 1
- out_gain: float32 [4096], P('head'), may hold values from 0.5 to 1.5
Outputs:
- layer_out: bfloat16 [16384, 4096], P('ctx', 'head')
All inputs are finite; a program needn't handle non-finite values.
Results may differ from a plain program's by a relative error of at most 0.02.
Values may be sent and summed in bfloat16 or wider, within the bound.
A program may use at most 128 MiB of HBM per device.

v0:
```python
import math

import jax
import jax.numpy as jnp
import numpy as np
from jax import lax
from jax.sharding import PartitionSpec as P

DH = 128
DK = 128
SPAN = 128


EPS = 1e-06


def partner_2(value, axis, stride):
    mask = 2**stride
    pairs = [(source, source ^ mask) for source in range(lax.axis_size(axis))]
    return lax.ppermute(value, axis, pairs)


def unit_rows(values):
    scale = lax.rsqrt(jnp.mean(values * values, axis=-1, keepdims=True) + EPS)
    return values * scale / math.sqrt(values.shape[-1])


def local(tokens, pair_weight, value_weight, output_weight, level_index, level_table, out_gain):
    row_count = tokens.shape[0]
    local_width = value_weight.shape[1]
    local_heads = local_width // DH
    portion = lax.all_gather(tokens, "head", axis=1, tiled=True)
    paired = jnp.dot(portion, pair_weight, preferred_element_type=jnp.float32)
    values = jnp.dot(portion, value_weight, preferred_element_type=jnp.float32)
    queries = unit_rows(paired[:, :DK]).astype(jnp.bfloat16)
    keys_all = unit_rows(paired[:, DK:]).astype(jnp.bfloat16)
    values = values.astype(jnp.bfloat16)
    blocks = row_count // SPAN
    local_bits = blocks.bit_length() - 1
    ctx_bits = lax.axis_size("ctx").bit_length() - 1
    device = lax.axis_index("ctx")
    table_ids = jnp.arange(level_table.shape[1], dtype=jnp.int32)
    onehot = (level_index[:, :, None] == table_ids[None, None, :]).astype(jnp.float32)
    mixing = jnp.einsum("tln,lnh->tlh", onehot, level_table, precision=lax.Precision.HIGHEST)
    query_blocks = queries.reshape(blocks, SPAN, DK)
    key_blocks = keys_all.reshape(blocks, SPAN, DK)
    value_blocks = values.reshape(blocks, SPAN, local_heads, DH)
    scores = jnp.einsum(
        "ncd,ned->nce", query_blocks, key_blocks, preferred_element_type=jnp.float32
    )
    causal = jnp.arange(SPAN)[:, None] >= jnp.arange(SPAN)[None, :]
    scores = jnp.where(causal[None], scores, 0.0).astype(jnp.bfloat16)
    result = jnp.einsum("nce,nehv->nchv", scores, value_blocks, preferred_element_type=jnp.float32)
    result = result.reshape(row_count, local_heads, DH) * mixing[:, 0, :, None]
    states = jnp.einsum(
        "ncd,nchv->nhdv", key_blocks, value_blocks, preferred_element_type=jnp.float32
    )
    selector = np.zeros((local_bits, blocks, blocks), np.float32)
    for level_bit in range(local_bits):
        block_width = 1 << level_bit
        for block_id in range(blocks):
            if block_id >> level_bit & 1:
                block_top = block_id >> level_bit << level_bit
                selector[level_bit, block_id, block_top - block_width : block_top] = 1.0
    buckets = jnp.einsum(
        "bij,jhdv->bihdv", jnp.asarray(selector), states, precision=lax.Precision.HIGHEST
    )
    buckets = buckets.astype(jnp.bfloat16)
    readout = jnp.einsum(
        "icd,bihdv->icbhv", query_blocks, buckets, preferred_element_type=jnp.float32
    )
    readout = readout.reshape(row_count, local_bits, local_heads, DH)
    result = result + jnp.sum(readout * mixing[:, 1 : 1 + local_bits, :, None], axis=1)
    totals = jnp.sum(states, axis=0)
    group_sum = totals
    level_states = []
    for level_bit in range(ctx_bits):
        partner = partner_2(group_sum.astype(jnp.bfloat16), "ctx", level_bit).astype(
            group_sum.dtype
        )
        present = (device >> level_bit & 1).astype(jnp.float32)
        level_states.append(partner * present)
        group_sum = group_sum + partner
    remote = jnp.stack(level_states)
    remote = remote.astype(jnp.bfloat16)
    far_readout = jnp.einsum("td,bhdv->tbhv", queries, remote, preferred_element_type=jnp.float32)
    result = result + jnp.sum(far_readout * mixing[:, 1 + local_bits :, :, None], axis=1)
    normed = result * lax.rsqrt(jnp.mean(result * result, axis=-1, keepdims=True) + EPS)
    normed = normed * out_gain.reshape(local_heads, DH)
    hidden = normed.reshape(row_count, local_width).astype(jnp.bfloat16)
    partial_value = jnp.dot(hidden, output_weight, preferred_element_type=jnp.float32)
    return lax.psum_scatter(
        partial_value.astype(jnp.bfloat16), "head", scatter_dimension=1, tiled=True
    )


def solution(mesh):
    return jax.shard_map(
        local,
        mesh=mesh,
        in_specs=(
            P("ctx", "head"),
            P(),
            P(None, "head"),
            P("head", None),
            P("ctx", None),
            P(None, None, "head"),
            P("head"),
        ),
        out_specs=P("ctx", "head"),
        check_vma=False,
    )
```

profile of v0, /device:TPU:7, one launch (start us, length us, event | category | flops | bytes accessed | tf_op | source)
XLA Modules:
  0.0 201.0 jit_solution(6517945876709319580)
XLA Ops:
  9.8 49.8 %all-gather.2.cloned.1.call-done = bf16[512,4096]{1,0:T(8,128)(2,1)} async-done(((bf16[512,1024]{1,0:T(8,128)(2,1)}), bf16[512,4096]{1,0:T(8,128)(2,1)}) %all-gather.2.cloned.1.call-update) | async-done | bytes 4194320 | tf_op jit(solution)/shard_map/all_gather | solution.py:32
  59.6 3.6 %fusion.32 = f32[512,256]{1,0:T(8,128)S(1)} fusion(bf16[512,4096]{1,0:T(8,128)(2,1)} %all-gather.2.cloned.1.call-done, bf16[4096,256]{1,0:T(8,128)(2,1)S(1)} %copy-done), kind=kOutput, calls=%fused_computation.64 | convolution fusion | flops 1073741824 | bytes 6815744 | tf_op jit(solution)/shard_map/dot_general | solution.py:33
  63.4 7.0 %fusion.4 = bf16[64,8,8,128]{3,1,2,0:T(8,128)(2,1)S(1)} fusion(bf16[512,4096]{1,0:T(8,128)(2,1)S(1)} %copy-done.9, bf16[4096,1024]{1,0:T(8,128)(2,1)} %param.10), kind=kOutput, calls=%fused_computation.14 | convolution fusion | flops 4295491584 | bytes 13631488 | tf_op jit(solution)/shard_map/dot_general | solution.py:34
  71.8 1.8 bitcast_reduce_fusion
  74.6 2.1 %copy.50 = f32[4,8,128,128,1]{3,0,4,2,1:T(4,128)S(1)} copy(f32[4,8,128,128,1]{2,3,1,0,4:T(8,128)} %bitcast.111) | data formatting | bytes 4194304 | tf_op jit(solution)/shard_map/ncd,nchv->nhdv/transpose | solution.py:55
  76.7 6.9 %convert_bitcast_fusion = bf16[2,4,8,128,128]{4,1,0,3,2:T(4,128)(2,1)S(1)} fusion(f32[4,8,128,128,1]{3,0,4,2,1:T(4,128)S(1)} %copy.50, f32[2,4,4,1,1]{2,1,0,4,3:T(4,128)S(1)} %copy-done.8), kind=kOutput, calls=%fused_computation.12 | convolution fusion | flops 51380224 | bytes 4194432 | tf_op jit(solution)/shard_map/bij,jhdv->bihdv/dot_general | solution.py:65
  85.0 1.3 multiply_reduce_fusion.1
  86.3 1.8 copy.45
  88.1 2.6 %copy.40 = f32[4,128,8,128]{3,2,1,0:T(8,128)} copy(f32[4,128,8,128]{3,1,2,0:T(8,128)S(1)} %multiply_reduce_fusion.1) | data formatting | bytes 4194304 | tf_op jit(solution)/shard_map/reduce_sum | solution.py:73
  90.6 1.9 collective-permute-done.1
  94.5 1.9 fusion.6
  96.4 1.9 copy.34
  98.2 3.8 %collective-permute-done.2 = bf16[8,128,128]{2,1,0:T(8,128)(2,1)S(1)} collective-permute-done((bf16[8,128,128]{2,1,0:T(8,128)(2,1)}, bf16[8,128,128]{2,1,0:T(8,128)(2,1)S(1)}, u32[]{:S(2)}, u32[]{:S(2)}) %collective-permute-start.2) | collective-permute-done | bytes 262176 | tf_op jit(solution)/shard_map/ppermute | solution.py:20
  102.2 1.3 collective-permute-start.3
  103.7 4.7 %collective-permute-done.3 = bf16[8,128,128]{2,1,0:T(8,128)(2,1)S(1)} collective-permute-done((bf16[8,128,128]{2,1,0:T(8,128)(2,1)S(1)}, bf16[8,128,128]{2,1,0:T(8,128)(2,1)S(1)}, u32[]{:S(2)}, u32[]{:S(2)}) %collective-permute-start.3) | collective-permute-done | bytes 262176 | tf_op jit(solution)/shard_map/ppermute | solution.py:20
  108.5 3.0 %collective-permute-start.4 = (bf16[8,128,128]{2,1,0:T(8,128)(2,1)S(1)}, bf16[8,128,128]{2,1,0:T(8,128)(2,1)S(1)}, u32[]{:S(2)}, u32[]{:S(2)}) collective-permute-start(bf16[8,128,128]{2,1,0:T(8,128)(2,1)S(1)} %fusion.13), channel_id=1, source_target_pairs={{0,64},{4,68},{8,72},{12,76},{16,80},{20,84},{24,88},{28,92},{32,9... | collective-permute-start | bytes 786440 | tf_op jit(solution)/shard_map/ppermute | solution.py:20
  111.7 3.8 %collective-permute-done.4 = bf16[8,128,128]{2,1,0:T(8,128)(2,1)S(1)} collective-permute-done((bf16[8,128,128]{2,1,0:T(8,128)(2,1)S(1)}, bf16[8,128,128]{2,1,0:T(8,128)(2,1)S(1)}, u32[]{:S(2)}, u32[]{:S(2)}) %collective-permute-start.4) | collective-permute-done | bytes 262176 | tf_op jit(solution)/shard_map/ppermute | solution.py:20
  115.6 4.8 %multiply_reduce_fusion = f32[512,8,128]{2,0,1:T(8,128)} fusion(f32[512,5,8]{0,2,1:T(8,128)S(1)} %slice-done, bf16[5,8,128,128]{3,2,1,0:T(8,128)(2,1)S(1)} %fusion.17, bf16[512,128]{1,0:T(8,128)(2,1)S(1)} %get-tuple-element.7), kind=kOutput, calls=%fused_computation | convolution fusion | flops 675807232 | bytes 3620864 | tf_op jit(solution)/shard_map/td,bhdv->tbhv/dot_general | solution.py:86
  120.3 2.9 %copy.43 = f32[512,8,128]{0,2,1:T(8,128)} copy(f32[512,8,128]{2,0,1:T(8,128)} %multiply_reduce_fusion) | data formatting | bytes 4194304 | tf_op jit(solution)/shard_map/reduce_sum | solution.py:87
  123.2 2.9 %copy.47 = f32[4,128,8,128]{1,3,2,0:T(8,128)} copy(f32[4,128,8,128]{3,1,0,2:T(8,128)} %bitcast.112) | data formatting | bytes 4194304 | tf_op jit(solution)/shard_map/reduce_sum | solution.py:87
  126.1 3.0 %multiply_reduce_fusion.2 = f32[4,128,8]{1,2,0:T(8,128)S(1)} fusion(f32[4,128,8,128]{1,3,2,0:T(8,128)} %copy.47, f32[4,128,8,128]{1,3,2,0:T(8,128)} %copy.45, f32[4,128,8]{1,2,0:T(8,128)S(1)} %get-tuple-element.10, f32[4,128,1024]{1,2,0:S(1)} %fusion.6), kind=kLoop, calls=%fused_computation.11 | loop fusion | flops 2617344 | bytes 6324224 | tf_op jit(solution)/shard_map/reduce_sum | solution.py:88
  129.3 2.0 copy.44
  133.5 10.3 %convolution_convert_fusion = bf16[512,4096]{1,0:T(8,128)(2,1)} fusion(bf16[1024,4096]{1,0:T(8,128)(2,1)} %param.11, f32[64,8,8,128]{3,2,1,0:T(8,128)S(1)} %bitcast.114, f32[512,1024]{1,0:T(8,128)S(1)} %copy.44, f32[64,8,8,128]{3,2,1,0:T(8,128)S(1)} %bitcast.116, f32[64,8,8,128]{3,2,1,0:T(8,128)S(1)} %bitcast.115, f32[64,8,8,128]{3,2,1,0:T(8,128)S(1)} %bitcast.117, ...), kind=kOutput, calls=%fused_computation.1 | convolution fusion | flops 4300210176 | bytes 23072768 | tf_op jit(solution)/shard_map/dot_general | solution.py:91
  143.8 50.4 %reduce-scatter.2.cloned.1.call-done = bf16[512,1024]{1,0:T(8,128)(2,1)} async-done(((bf16[512,4096]{1,0:T(8,128)(2,1)}), bf16[512,1024]{1,0:T(8,128)(2,1)}) %reduce-scatter.2.cloned.1.call-update) | async-done | bytes 1048592 | tf_op jit(solution)/shard_map/reduce_scatter | solution.py:92
  (56 shorter events, 12.0 us)
Async XLA Ops:
  6.5 53.1 %copy-start = (bf16[4096,256]{1,0:T(8,128)(2,1)S(1)}, bf16[4096,256]{1,0:T(8,128)(2,1)}, u32[]{:S(2)}) copy-start(bf16[4096,256]{1,0:T(8,128)(2,1)} %param.9) | copy-start | bytes 6291460
  6.5 53.1 %all-gather.2.cloned.1.call-start = ((), (), s32[]{:S(2)}) async-start(), calls=%async_computation.1 | async-start | bytes 5242880 | tf_op jit(solution)/shard_map/all_gather | solution.py:32
  7.3 186.9 %reduce-scatter.2.cloned.1.call-start = ((), (), s32[]{:S(2)}) async-start(), calls=%async_computation.2 | async-start | bytes 5242880 | tf_op jit(solution)/shard_map/reduce_scatter | solution.py:92
  8.3 76.7 %copy-start.7 = (f32[512,8,8]{0,2,1:T(8,128)}, f32[512,8,8]{0,2,1:T(8,128)S(1)}, u32[]{:S(2)}) copy-start(f32[512,8,8]{0,2,1:T(8,128)S(1)} %convolution_bitcast_fusion) | copy-start | bytes 393220
  59.6 3.8 %copy-start.9 = (bf16[512,4096]{1,0:T(8,128)(2,1)S(1)}, bf16[512,4096]{1,0:T(8,128)(2,1)}, u32[]{:S(2)}) copy-start(bf16[512,4096]{1,0:T(8,128)(2,1)} %all-gather.2.cloned.1.call-done) | copy-start | bytes 12582916
  71.5 3.1 %copy-start.2 = (bf16[4,128,8,128]{1,3,2,0:T(8,128)(2,1)}, bf16[4,128,8,128]{1,3,2,0:T(8,128)(2,1)S(1)}, u32[]{:S(2)}) copy-start(bf16[4,128,8,128]{1,3,2,0:T(8,128)(2,1)S(1)} %copy.33) | copy-start | bytes 3145732
  71.8 2.0 %copy-start.5 = (bf16[512,128]{1,0:T(8,128)(2,1)}, bf16[512,128]{1,0:T(8,128)(2,1)S(1)}, u32[]{:S(2)}) copy-start(bf16[512,128]{1,0:T(8,128)(2,1)S(1)} %get-tuple-element.8) | copy-start | bytes 393220
  73.8 9.8 %collective-permute-start = (bf16[8,128,128]{2,1,0:T(8,128)(2,1)S(1)}, bf16[8,128,128]{2,1,0:T(8,128)(2,1)S(1)}, u32[]{:S(2)}, u32[]{:S(2)}) collective-permute-start(bf16[8,128,128]{2,1,0:T(8,128)(2,1)S(1)} %convert_element_type.77), channel_id=1, source_target_pairs={{0,4},{4,0},{8,12},{12,8},{16,20},{20,16},{24,28},{28,24},{32,36},... | collective-permute-start | bytes 786440 | tf_op jit(solution)/shard_map/ppermute | solution.py:20
  74.6 2.1 %copy-start.8 = (f32[2,4,4,1,1]{2,1,0,4,3:T(4,128)S(1)}, f32[2,4,4,1,1]{2,1,0,4,3:T(4,128)}, u32[]{:S(2)}) copy-start(f32[2,4,4,1,1]{2,1,0,4,3:T(4,128)} %constant.34) | copy-start | bytes 388
  84.4 8.1 %collective-permute-start.1 = (bf16[8,128,128]{2,1,0:T(8,128)(2,1)}, bf16[8,128,128]{2,1,0:T(8,128)(2,1)S(1)}, u32[]{:S(2)}, u32[]{:S(2)}) collective-permute-start(bf16[8,128,128]{2,1,0:T(8,128)(2,1)} %fusion.14), channel_id=1, source_target_pairs={{0,8},{4,12},{8,0},{12,4},{16,24},{20,28},{24,16},{28,20},{32,40},... | collective-permute-start | bytes 786440 | tf_op jit(solution)/shard_map/ppermute | solution.py:20
  93.3 8.7 %collective-permute-start.2 = (bf16[8,128,128]{2,1,0:T(8,128)(2,1)}, bf16[8,128,128]{2,1,0:T(8,128)(2,1)S(1)}, u32[]{:S(2)}, u32[]{:S(2)}) collective-permute-start(bf16[8,128,128]{2,1,0:T(8,128)(2,1)} %fusion.31), channel_id=1, source_target_pairs={{0,16},{4,20},{8,24},{12,28},{16,0},{20,4},{24,8},{28,12},{32,48},... | collective-permute-start | bytes 786440 | tf_op jit(solution)/shard_map/ppermute | solution.py:20
  102.2 6.2 %collective-permute-start.3 = (bf16[8,128,128]{2,1,0:T(8,128)(2,1)S(1)}, bf16[8,128,128]{2,1,0:T(8,128)(2,1)S(1)}, u32[]{:S(2)}, u32[]{:S(2)}) collective-permute-start(bf16[8,128,128]{2,1,0:T(8,128)(2,1)S(1)} %fusion.15), channel_id=1, source_target_pairs={{0,32},{4,36},{8,40},{12,44},{16,48},{20,52},{24,56},{28,60},{32,0... | collective-permute-start | bytes 786440 | tf_op jit(solution)/shard_map/ppermute | solution.py:20
  103.6 12.0 %slice-start = ((f32[512,8,8]{0,2,1:T(8,128)}), f32[512,5,8]{0,2,1:T(8,128)S(1)}, s32[]{:S(2)}) async-start(f32[512,8,8]{0,2,1:T(8,128)} %copy-done.7), calls=%async_computation.3 | async-start | bytes 163840 | tf_op jit(solution)/shard_map/slice | solution.py:87
  108.5 6.9 %collective-permute-start.4 = (bf16[8,128,128]{2,1,0:T(8,128)(2,1)S(1)}, bf16[8,128,128]{2,1,0:T(8,128)(2,1)S(1)}, u32[]{:S(2)}, u32[]{:S(2)}) collective-permute-start(bf16[8,128,128]{2,1,0:T(8,128)(2,1)S(1)} %fusion.13), channel_id=1, source_target_pairs={{0,64},{4,68},{8,72},{12,76},{16,80},{20,84},{24,88},{28,92},{32,9... | collective-permute-start | bytes 786440 | tf_op jit(solution)/shard_map/ppermute | solution.py:20
  129.3 2.6 %copy-start.6 = (f32[512,8]{1,0:T(8,128)S(1)}, f32[512,8]{1,0:T(8,128)}, u32[]{:S(2)}) copy-start(f32[512,8]{1,0:T(8,128)} %copy.35) | copy-start | bytes 49156
  131.3 1.6 copy-start.3
  131.3 2.2 %copy-start.4 = (f32[4,128,8,128]{3,2,1,0:T(8,128)S(1)}, f32[4,128,8,128]{3,2,1,0:T(8,128)}, u32[]{:S(2)}) copy-start(f32[4,128,8,128]{3,2,1,0:T(8,128)} %copy.34) | copy-start | bytes 6291460
  131.3 2.2 %copy-start.10 = (f32[1024]{0:T(1024)S(1)}, f32[1024]{0:T(1024)}, u32[]{:S(2)}) copy-start(f32[1024]{0:T(1024)} %param.14) | copy-start | bytes 12292
  143.8 50.4 %copy-start.1 = (bf16[4096,256]{1,0:T(8,128)(2,1)S(1)}, bf16[4096,256]{1,0:T(8,128)(2,1)}, u32[]{:S(2)}) copy-start(bf16[4096,256]{1,0:T(8,128)(2,1)} %param.9) | copy-start | bytes 6291460
Sparse Core Ops, SparseCore 0:
  9.0 50.5 all-gather.1
  144.0 50.1 reduce-scatter.1
where the time goes:
time: 202 us; the launch traced here: 201 us
  waiting for transfers between devices  115 us (57%)
  matrix products  38.5 us (19%)
  local copies, waits for them, and re-layouts  20.6 us (10%)
  between operations  13.7 us (7%)
  starting transfers between devices  6.83 us (3%)
  other arithmetic  6.33 us (3%)
    reduce_scatter x1, waiting for transfers between devices, local(): lax.psum_scatter(partial_value.astype(jnp.bfloat16), 'head', scatter_dime...  50.4 us
    all_gather x1, waiting for transfers between devices, local(): portion = lax.all_gather(tokens, 'head', axis=1, tiled=True)  49.8 us
    ppermute x5, waiting for transfers between devices, partner_2(): return lax.ppermute(value, axis, pairs)  14.2 us
    dot_general x1, matrix products, local(): jnp.dot(hidden, output_weight, preferred_element_type=jnp.float32)  10.3 us
    reduce_sum x3, local copies, waits for them, and re-layouts, local(): jnp.sum(far_readout * mixing[:, 1 + local_bits:, :, None], axis=1)  7.8 us
    dot_general x1, matrix products, local(): values = jnp.dot(portion, value_weight, preferred_element_type=jnp.float32)  7.02 us
    dot_general x1, matrix products, local(): jnp.einsum('bij,jhdv->bihdv', jnp.asarray(selector), states, precision=la...  6.89 us
    ppermute x5, starting transfers between devices, partner_2(): return lax.ppermute(value, axis, pairs)  6.79 us
  transfers between devices with their start and end apart: 7, of which 6 were waited for; matrix products, arithmetic and copies ran while one was open for 11% of the time, Pallas kernels for 0%

commit v1 on v0

v1 whole, which is shorter than its diff:
```python
import math

import jax
import jax.numpy as jnp
from jax import lax
from jax.experimental import pallas as pl
from jax.experimental.pallas import tpu as pltpu
from jax.sharding import PartitionSpec as P

DH = 128
DK = 128
SPAN = 128
EPS = 1e-06
CHUNKS = 4
WIDTH = 1024
TILE = 256
CHIPS = 16
MESH = pl.DeviceIdType.MESH
BF = jnp.bfloat16
F32 = jnp.float32


def dot(a, b):
    return jnp.dot(a, b, preferred_element_type=F32)


def unit_rows(values):
    scale = lax.rsqrt(jnp.mean(values * values, axis=-1, keepdims=True) + EPS)
    return values * scale / math.sqrt(values.shape[-1])


def kernel(
    tok, pw, vw, ow, lidx, ltab, gain, out,
    full, wv, owv, acc, mixn, q, s01, s0b, s2b, tot, tb, tpeer, mixed,
    cb, r1, sb, r2, r2o, hid, popp, rpopp, psum, rpsum, pown,
    w_sem, own_send, own_recv, fwd_send, fwd_recv, core_sem, one_sem, two_sem, swap_sem,
    opp_send, opp_recv, plain_send, plain_recv, sum_send, sum_recv,
):
    me = lax.axis_index("head")
    ctx = lax.axis_index("ctx")
    right = lax.rem(me + 1, 4)
    left = lax.rem(me + 3, 4)
    opposite = lax.rem(me + 2, 4)
    core = lax.rem(ctx, 2)
    chip = lax.div(ctx, 2)
    other = ctx + 1 - 2 * core
    bits = [lax.rem(lax.div(chip, 1 << i), 2) for i in range(4)]
    count = bits[0] + bits[1] + bits[2] + bits[3]

    def remote(src, dst, send, recv, **axes):
        return pltpu.make_async_remote_copy(
            src_ref=src, dst_ref=dst, send_sem=send, recv_sem=recv,
            device_id=axes, device_id_type=MESH,
        )

    loads = [
        pltpu.make_async_copy(pw, wv.at[4], w_sem.at[4]),
    ]
    for n in range(4):
        loads.append(pltpu.make_async_copy(vw.at[:, pl.ds(n * TILE, TILE)], wv.at[n], w_sem.at[n]))
    tok_load = pltpu.make_async_copy(tok, full.at[me], w_sem.at[5])
    ow_loads = [
        pltpu.make_async_copy(ow.at[:, pl.ds(t * TILE, TILE)], owv.at[t], w_sem.at[6 + t])
        for t in range(16)
    ]

    barrier = pltpu.get_barrier_semaphore()
    for peer in (left, right):
        pl.semaphore_signal(barrier, inc=1, device_id={"head": peer}, device_id_type=MESH)
    pl.semaphore_signal(barrier, inc=1, device_id={"ctx": other}, device_id_type=MESH)

    def greet(d, carry):
        dest = lax.rem(chip + d, CHIPS) * 2 + core
        pl.semaphore_signal(barrier, inc=1, device_id={"ctx": dest}, device_id_type=MESH)
        return carry

    lax.fori_loop(1, CHIPS, greet, 0)
    tok_load.start()
    for load in loads:
        load.start()
    pl.semaphore_wait(barrier, 3 + CHIPS - 1)

    peers = (right, left)
    HALF = SPAN // 2

    def own(r, d):
        rows = pl.ds(r * SPAN, SPAN)
        return remote(tok.at[rows], full.at[me, rows], own_send.at[d, r], own_recv.at[d, r], head=peers[d])

    def own_in(r, d):
        rows = pl.ds(r * SPAN, SPAN)
        slot = (left, right)[d]
        return remote(tok.at[rows], full.at[slot, rows], own_send.at[d, r], own_recv.at[d, r], head=peers[d])

    def forward(r, d):
        rows = pl.ds(r * SPAN + d * HALF, HALF)
        slot = (left, right)[d]
        return remote(full.at[slot, rows], full.at[slot, rows], fwd_send.at[d, r], fwd_recv.at[d, r], head=peers[d])

    def forward_in(r, d):
        rows = pl.ds(r * SPAN + d * HALF, HALF)
        return remote(full.at[opposite, rows], full.at[opposite, rows], fwd_send.at[d, r], fwd_recv.at[d, r], head=peers[d])

    for r in range(2):
        for d in range(2):
            own(r, d).start()

    level_of = lax.broadcasted_iota(jnp.int32, (8, 128), 0)
    lane = lax.broadcasted_iota(jnp.int32, (8, 128), 1)
    spread = jnp.where(level_of == lane // 16, 1.0, 0.0).astype(BF)
    wanted = dot(lidx[...].astype(F32).astype(BF), spread)
    entry = lax.broadcasted_iota(jnp.int32, (CHUNKS * SPAN, 128), 1) % 16
    onehot = jnp.where(wanted == entry.astype(F32), 1.0, 0.0)
    row = lax.broadcasted_iota(jnp.int32, (128, 128), 0)
    column = lax.broadcasted_iota(jnp.int32, (128, 128), 1)
    for n in range(4):
        first = jnp.broadcast_to(ltab[:, 2 * n : 2 * n + 1], (128, 128))
        second = jnp.broadcast_to(ltab[:, 2 * n + 1 : 2 * n + 2], (128, 128))
        table = jnp.where(row // 16 == column // 2, jnp.where(column % 2 == 0, first, second), 0.0)
        mixn[n] = jnp.dot(onehot, table, preferred_element_type=F32, precision=lax.Precision.HIGHEST)
    r2[4] = jnp.zeros((CHIPS, 16, TILE), BF)
    r2o[4] = jnp.zeros((CHIPS, 16, TILE), BF)

    def weighted(value, n, rows, level):
        parts = []
        for h in range(2):
            w = mixn[n, rows, 2 * level + h : 2 * level + h + 1]
            parts.append(value[:, h * DH : (h + 1) * DH] * w)
        return jnp.concatenate(parts, axis=1)

    for load in loads:
        load.wait()
    tok_load.wait()
    for load in ow_loads:
        load.start()

    def first_part(r):
        rows = pl.ds(r * SPAN, SPAN)

        def body(n, carry):
            total = None
            for slot in (me, left, right):
                term = dot(full[slot, rows, :], wv[n, pl.ds(pl.multiple_of(slot * WIDTH, WIDTH), WIDTH), :])
                total = term if total is None else total + term
            acc[r % 2, n] = total
            return carry

        lax.fori_loop(0, 5, body, 0)

    def second_part(r):
        rows = pl.ds(r * SPAN, SPAN)
        where = pl.ds(pl.multiple_of(opposite * WIDTH, WIDTH), WIDTH)
        block = full[opposite, rows, :]
        paired = acc[r % 2, 4] + dot(block, wv[4, where, :])
        query = unit_rows(paired[:, :DK]).astype(BF)
        key_t = unit_rows(paired[:, DK:]).T.astype(BF)
        q[rows, :] = query
        scores = dot(query, key_t)
        t = lax.broadcasted_iota(jnp.int32, (SPAN, SPAN), 0)
        s = lax.broadcasted_iota(jnp.int32, (SPAN, SPAN), 1)
        scores = jnp.where(t >= s, scores, 0.0).astype(BF)

        def body(n, carry):
            value = (acc[r % 2, n] + dot(full[opposite, rows, :], wv[n, where, :])).astype(BF)
            result = weighted(dot(scores, value), n, rows, 0)
            state = dot(key_t, value)
            if r == 0:
                s01[n] = state
                s0b[n] = state.astype(BF)
            elif r == 1:
                result += weighted(dot(query, s0b[n]), n, rows, 1)
                s01[n] = s01[n] + state
            elif r == 2:
                result += weighted(dot(query, s01[n].astype(BF)), n, rows, 2)
                s2b[n] = state.astype(BF)
                tot[n] = s01[n] + state
            else:
                result += weighted(dot(query, s2b[n]), n, rows, 1)
                result += weighted(dot(query, s01[n].astype(BF)), n, rows, 2)
                total = tot[n] + state
                tot[n] = total
                tb[n] = total.astype(BF)
            mixed[n, rows, :] = result
            return carry

        lax.fori_loop(0, 4, body, 0)

    for r in range(CHUNKS):
        for d in range(2):
            own_in(r, d).wait_recv()
            forward(r, d).start()
        if r + 2 < CHUNKS:
            for d in range(2):
                own(r + 2, d).start()
        first_part(r)
        if r > 0:
            for d in range(2):
                forward_in(r - 1, d).wait_recv()
            second_part(r - 1)
    for d in range(2):
        forward_in(CHUNKS - 1, d).wait_recv()
    second_part(CHUNKS - 1)

    core_copy = remote(tb, tpeer, core_sem.at[0], core_sem.at[1], ctx=other)
    core_copy.start()
    core_copy.wait_recv()
    for m in range(2):
        n = 2 * core + m
        both = tot[n] + tpeer[n].astype(F32)
        cb[m * 8 : (m + 1) * 8] = both.astype(BF).reshape(8, 16, TILE)

    def piece(d, carry):
        dest = lax.rem(chip + d, CHIPS)
        remote(cb.at[dest], r1.at[chip], one_sem.at[0], one_sem.at[1], ctx=dest * 2 + core).start()
        return carry

    lax.fori_loop(1, CHIPS, piece, 0)
    r1[chip] = cb[chip]
    others = pl.ds(0, CHIPS - 1)
    remote(cb.at[others], r1.at[others], one_sem.at[0], one_sem.at[1], ctx=other).wait_recv()

    piece_of = [r1[c].astype(F32) for c in range(CHIPS)]
    pair = [piece_of[4 * z] + piece_of[4 * z + 1] for z in range(4)]
    line = [pair[z] + (piece_of[4 * z + 2] + piece_of[4 * z + 3]) for z in range(4)]
    lower = line[0] + line[1]
    for c in range(CHIPS):
        z, x = c // 4, c % 4
        slot = 0
        for bit, value in ((x & 1, piece_of[c - 1]), (x & 2, pair[z]), (z & 1, line[z - 1]), (z & 2, lower)):
            if bit:
                sb[4 * c + slot] = value.astype(BF)
                slot += 1

    def spread_sums(d, carry):
        dest = lax.rem(chip + d, CHIPS)
        dest_count = sum(lax.rem(lax.div(dest, 1 << i), 2) for i in range(4))
        for j in range(1, 5):
            @pl.when(dest_count == j)
            def _():
                remote(
                    sb.at[pl.ds(4 * dest, j)], r2.at[pl.ds(0, j), chip],
                    two_sem.at[0], two_sem.at[1], ctx=dest * 2 + core,
                ).start()
        return carry

    lax.fori_loop(1, CHIPS, spread_sums, 0)
    for j in range(1, 5):
        @pl.when(count == j)
        def _():
            for s in range(j):
                r2[s, chip] = sb[4 * chip + s]
            here = r2.at[pl.ds(0, j), pl.ds(0, CHIPS - 1)]
            remote(here, here, two_sem.at[0], two_sem.at[1], ctx=other).wait_recv()
            remote(r2.at[pl.ds(0, j)], r2o.at[pl.ds(0, j)], swap_sem.at[0], swap_sem.at[1], ctx=other).start()

    rank = 0
    slots = []
    for i in range(4):
        slots.append(bits[i] * rank + (1 - bits[i]) * 4)
        rank = rank + bits[i]
    core_on = core.astype(F32)

    def far_tile(r, n, m, source):
        rows = pl.ds(r * SPAN, SPAN)
        query = q[rows, :]
        x = mixed[n, rows, :]
        x += weighted(dot(query, tpeer[n]) * core_on, n, rows, 3)
        for i in range(4):
            bucket = source[slots[i], pl.ds(pl.multiple_of(m * 8, 8), 8)].reshape(128, TILE)
            x += weighted(dot(query, bucket), n, rows, 4 + i)
        for h in range(2):
            one = x[:, h * DH : (h + 1) * DH]
            one = one * lax.rsqrt(jnp.mean(one * one, axis=-1, keepdims=True) + EPS)
            one = one * gain[2 * n + h]
            hid[rows, pl.ds(pl.multiple_of(n * TILE + h * DH, DH), DH)] = one.astype(BF)

    def far(r):
        def near_half(m, carry):
            far_tile(r, 2 * core + m, m, r2)
            return carry

        def far_half(m, carry):
            far_tile(r, 2 - 2 * core + m, m, r2o)
            return carry

        lax.fori_loop(0, 2, near_half, 0)
        if r == 0:
            for j in range(1, 5):
                @pl.when(count == j)
                def _():
                    copy = remote(r2.at[pl.ds(0, j)], r2o.at[pl.ds(0, j)], swap_sem.at[0], swap_sem.at[1], ctx=other)
                    copy.wait_recv()
        lax.fori_loop(0, 2, far_half, 0)

    def opp_copy(r, d):
        return remote(popp.at[r, d], rpopp.at[r, d], opp_send.at[d, r], opp_recv.at[d, r], head=peers[d])

    def plain_copy(r, d):
        half = pl.ds(2 - 2 * d, 2)
        return remote(psum.at[r, d, half], rpsum.at[r, d, half], plain_send.at[d, r], plain_recv.at[d, r], head=peers[d])

    def sum_copy(r, d):
        half = pl.ds(2 * d, 2)
        return remote(psum.at[r, d, half], rpsum.at[r, d, half], sum_send.at[d, r], sum_recv.at[d, r], head=peers[d])

    def project(r, dest, n):
        return dot(hid[pl.ds(r * SPAN, SPAN), :], owv[dest * 4 + n])

    def opposite_part(r):
        def body(n, carry):
            popp[r, lax.div(n, 2), lax.rem(n, 2)] = project(r, opposite, n).astype(BF)
            return carry

        lax.fori_loop(0, 4, body, 0)
        for d in range(2):
            opp_copy(r, d).start()

    def neighbour_part(r):
        for d in range(2):
            def body(n, carry):
                psum[r, d, n] = project(r, peers[d], n).astype(BF)
                return carry

            lax.fori_loop(0, 4, body, 0)
            plain_copy(r, d).start()

    def relay(r):
        for d in range(2):
            opp_copy(r, d).wait_recv()
            for m in range(2):
                n = 2 * d + m
                psum[r, d, n] = (psum[r, d, n].astype(F32) + rpopp[r, d, m].astype(F32)).astype(BF)
            sum_copy(r, d).start()

    def own_part(r):
        def body(n, carry):
            pown[r, n] = project(r, me, n).astype(BF)
            return carry

        lax.fori_loop(0, 4, body, 0)

    def finish(r):
        for d in range(2):
            plain_copy(r, d).wait_recv()
            sum_copy(r, d).wait_recv()
        for n in range(4):
            total = pown[r, n].astype(F32) + rpsum[r, 0, n].astype(F32) + rpsum[r, 1, n].astype(F32)
            out[pl.ds(r * SPAN, SPAN), n * TILE : (n + 1) * TILE] = total.astype(BF)

    for r in range(CHUNKS):
        far(r)
        if r == 0:
            for load in ow_loads:
                load.wait()
        opposite_part(r)
        if r > 0:
            relay(r - 1)
        neighbour_part(r)
        own_part(r)
    relay(CHUNKS - 1)
    for r in range(CHUNKS):
        finish(r)

    for r in range(CHUNKS):
        for d in range(2):
            own(r, d).wait_send()
            forward(r, d).wait_send()
            opp_copy(r, d).wait_send()
            plain_copy(r, d).wait_send()
            sum_copy(r, d).wait_send()
    core_copy.wait_send()
    remote(cb.at[others], r1.at[others], one_sem.at[0], one_sem.at[1], ctx=other).wait_send()
    for j in range(0, 5):
        @pl.when(count == j)
        def _():
            sent = sb.at[pl.ds(0, 32 - j)]
            remote(sent, sent, two_sem.at[0], two_sem.at[1], ctx=other).wait_send()
            if j:
                remote(r2.at[pl.ds(0, j)], r2o.at[pl.ds(0, j)], swap_sem.at[0], swap_sem.at[1], ctx=other).wait_send()


def local(tokens, pair_weight, value_weight, output_weight, level_index, level_table, out_gain):
    any_space = pl.BlockSpec(memory_space=pl.ANY)
    vmem = pl.BlockSpec(memory_space=pltpu.VMEM)
    rows = tokens.shape[0]
    dma = pltpu.SemaphoreType.DMA
    return pl.pallas_call(
        kernel,
        out_shape=jax.ShapeDtypeStruct((rows, WIDTH), BF),
        in_specs=[any_space] * 4 + [vmem] * 3,
        out_specs=vmem,
        scratch_shapes=[
            pltpu.VMEM((4, rows, WIDTH), BF),
            pltpu.VMEM((5, 4 * WIDTH, TILE), BF),
            pltpu.VMEM((16, WIDTH, TILE), BF),
            pltpu.VMEM((2, 5, SPAN, TILE), F32),
            pltpu.VMEM((4, rows, 128), F32),
            pltpu.VMEM((rows, DK), BF),
            pltpu.VMEM((4, DK, TILE), F32),
            pltpu.VMEM((4, DK, TILE), BF),
            pltpu.VMEM((4, DK, TILE), BF),
            pltpu.VMEM((4, DK, TILE), F32),
            pltpu.VMEM((4, DK, TILE), BF),
            pltpu.VMEM((4, DK, TILE), BF),
            pltpu.VMEM((4, rows, TILE), F32),
            pltpu.VMEM((CHIPS, 16, TILE), BF),
            pltpu.VMEM((CHIPS, 16, TILE), BF),
            pltpu.VMEM((4 * CHIPS, 16, TILE), BF),
            pltpu.VMEM((5, CHIPS, 16, TILE), BF),
            pltpu.VMEM((5, CHIPS, 16, TILE), BF),
            pltpu.VMEM((rows, WIDTH), BF),
            pltpu.VMEM((CHUNKS, 2, 2, SPAN, TILE), BF),
            pltpu.VMEM((CHUNKS, 2, 2, SPAN, TILE), BF),
            pltpu.VMEM((CHUNKS, 2, 4, SPAN, TILE), BF),
            pltpu.VMEM((CHUNKS, 2, 4, SPAN, TILE), BF),
            pltpu.VMEM((CHUNKS, 4, SPAN, TILE), BF),
            dma((22,)),
            dma((2, CHUNKS)),
            dma((2, CHUNKS)),
            dma((2, CHUNKS)),
            dma((2, CHUNKS)),
            dma((2,)),
            dma((2,)),
            dma((2,)),
            dma((2,)),
            dma((2, CHUNKS)),
            dma((2, CHUNKS)),
            dma((2, CHUNKS)),
            dma((2, CHUNKS)),
            dma((2, CHUNKS)),
            dma((2, CHUNKS)),
        ],
        compiler_params=pltpu.CompilerParams(
            collective_id=0, has_side_effects=True, vmem_limit_bytes=56 * 1024 * 1024
        ),
        name="layer",
    )(
        tokens, pair_weight, value_weight, output_weight, level_index,
        level_table.reshape(128, 8), out_gain.reshape(8, 1, 128),
    )


def solution(mesh):
    return jax.shard_map(
        local,
        mesh=mesh,
        in_specs=(
            P("ctx", "head"),
            P(),
            P(None, "head"),
            P("head", None),
            P("ctx", None),
            P(None, None, "head"),
            P("head"),
        ),
        out_specs=P("ctx", "head"),
        check_vma=False,
    )
```

time: 202 us -> 107 us (0.53)
  waiting for transfers between devices: 115 us -> 0 us
  Pallas kernels: 0 us -> 101 us
  matrix products: 38.5 us -> 0 us
  local copies, waits for them, and re-layouts: 20.6 us -> 5.27 us
  between operations: 13.7 us -> 0.01 us
  starting transfers between devices: 6.83 us -> 0 us
  other arithmetic: 6.33 us -> 0 us
    pallas_call x0 -> x1, Pallas kernels: none -> 101 us  [local(): pl.pallas_call(kernel, out_shape=jax.ShapeDtypeStruct((rows, WIDTH), BF),...]
    reduce_scatter x1 -> x0, waiting for transfers between devices: 50.4 us -> none  [local(): lax.psum_scatter(partial_value.astype(jnp.bfloat16), 'head', scatter_dime...]
    all_gather x1 -> x0, waiting for transfers between devices: 49.8 us -> none  [local(): portion = lax.all_gather(tokens, 'head', axis=1, tiled=True)]
    dot_general x8 -> x0, matrix products: 36.6 us -> none  [the longest x1 10.3 us: local(): jnp.dot(hidden, output_weight, preferred_element_type=jnp.float32)]
    ppermute x5 -> x0, waiting for transfers between devices: 14.2 us -> none  [partner_2(): return lax.ppermute(value, axis, pairs)]
    reduce_sum x6 -> x0, local copies, waits for them, and re-layouts: 12.4 us -> none  [the longest x3 7.8 us: local(): jnp.sum(far_readout * mixing[:, 1 + local_bits:, :, None], axis=1)]
    ppermute x5 -> x0, starting transfers between devices: 6.79 us -> none  [partner_2(): return lax.ppermute(value, axis, pairs)]
    unnamed x23 -> x3, local copies, waits for them, and re-layouts: 1.29 us -> 5.27 us
  transfers between devices with their start and end apart: 7 -> 0, of which waited for: 6 -> 0; matrix products, arithmetic and copies ran while one was open for 11% -> 0% of each run, Pallas kernels for 0% -> 0%
where the time goes in v1:
time: 107 us; the launch traced here: 106 us
  Pallas kernels  101 us (94%)
  local copies, waits for them, and re-layouts  5.27 us (5%)
    pallas_call x1, Pallas kernels, local(): pl.pallas_call(kernel, out_shape=jax.ShapeDtypeStruct((rows, WIDTH), BF),...  101 us
    unnamed x3, local copies, waits for them, and re-layouts  5.27 us

profile of v1, /device:TPU:7, one launch (start us, length us, event | category | flops | bytes accessed | tf_op | source)
XLA Modules:
  0.0 106.3 jit_solution(4958391767404677342)
XLA Ops:
  0.0 1.5 %copy.8 = f32[8,16,8]{2,1,0:T(8,128)} copy(f32[8,16,8]{1,2,0:T(8,128)} %param.12) | data formatting | bytes 8192 | tf_op args[5]
  1.5 1.6 %copy.9.lidx = s32[512,8]{1,0:T(8,128)} copy(s32[512,8]{0,1:T(8,128)} %param.11) | data formatting | bytes 32768 | tf_op args[4]
  3.0 101.0 %layer.1 = bf16[512,1024]{1,0:T(8,128)(2,1)} custom-call(bf16[512,1024]{1,0:T(8,128)(2,1)} %tok.1, bf16[4096,256]{1,0:T(8,128)(2,1)} %pw.1, bf16[4096,1024]{1,0:T(8,128)(2,1)} %vw.1, bf16[1024,4096]{1,0:T(8,128)(2,1)} %ow.1, s32[512,8]{1,0:T(8,128)} %copy.9.lidx, f32[128,8]{1,0:T(8,128)} %bitcast.2, f32[8,1,128]{2,1,0:T(1,128)} %bitcast.3), custom_call_target="tpu_custom_call" | custom-call | tf_op jit(solution)/shard_map/layer/pallas_call | solution.py:387
  104.0 2.3 %copy.11 = bf16[512,1024]{1,0:T(8,128)(2,1)} copy(bf16[512,1024]{1,0:T(8,128)(2,1)} %layer.1) | data formatting | bytes 2097152

commit v2 on v1

--- a/solution.py
+++ b/solution.py
@@ -31,9 +31,10 @@
 
 def kernel(
     tok, pw, vw, ow, lidx, ltab, gain, out,
-    full, wv, owv, acc, mixn, q, s01, s0b, s2b, tot, tb, tpeer, mixed,
-    cb, r1, sb, r2, r2o, hid, popp, rpopp, psum, rpsum, pown,
-    w_sem, own_send, own_recv, fwd_send, fwd_recv, core_sem, one_sem, two_sem, swap_sem,
+    full, wv, owv, acc, mixn, q, kt, last, s01, s0b, s2b, tot, tb, tpeer, mixed,
+    cb, r1, sb, r2, r2o, hid, popp, rpopp, psum, rpsum, pown, stage,
+    w_sem, own_send, own_recv, fwd_send, fwd_recv, core_send, core_recv, one_sem, pair_sem, two_send, two_recv,
+    swap_send, swap_recv, out_sem,
     opp_send, opp_recv, plain_send, plain_recv, sum_send, sum_recv,
 ):
     me = lax.axis_index("head")
@@ -45,7 +46,7 @@
     chip = lax.div(ctx, 2)
     other = ctx + 1 - 2 * core
     bits = [lax.rem(lax.div(chip, 1 << i), 2) for i in range(4)]
-    count = bits[0] + bits[1] + bits[2] + bits[3]
+    count = bits[1] + bits[2] + bits[3]
 
     def remote(src, dst, send, recv, **axes):
         return pltpu.make_async_remote_copy(
@@ -105,19 +106,21 @@
         for d in range(2):
             own(r, d).start()
 
-    level_of = lax.broadcasted_iota(jnp.int32, (8, 128), 0)
-    lane = lax.broadcasted_iota(jnp.int32, (8, 128), 1)
-    spread = jnp.where(level_of == lane // 16, 1.0, 0.0).astype(BF)
-    wanted = dot(lidx[...].astype(F32).astype(BF), spread)
-    entry = lax.broadcasted_iota(jnp.int32, (CHUNKS * SPAN, 128), 1) % 16
-    onehot = jnp.where(wanted == entry.astype(F32), 1.0, 0.0)
-    row = lax.broadcasted_iota(jnp.int32, (128, 128), 0)
-    column = lax.broadcasted_iota(jnp.int32, (128, 128), 1)
+    row = lax.broadcasted_iota(jnp.int32, (128, 8), 0)
+    spread = jnp.where(row // 16 == lax.broadcasted_iota(jnp.int32, (128, 8), 1), 1.0, 0.0).astype(BF)
+    wanted = dot(spread, lidx[...].astype(F32).astype(BF))
+    entry = lax.broadcasted_iota(jnp.int32, (128, CHUNKS * SPAN), 0) % 16
+    onehot = jnp.where(wanted == entry.astype(F32), 1.0, 0.0).T
+    exact = lax.Precision.HIGHEST
+    level_of = lax.broadcasted_iota(jnp.int32, (64, 128), 0) // 8
+    lane_level = lax.broadcasted_iota(jnp.int32, (64, 128), 1) // 16
+    placed = jnp.where(level_of == lane_level, jnp.concatenate([ltab[...]] * 8, axis=1), 0.0)
+    column = lax.broadcasted_iota(jnp.int32, (128, 64), 0)
+    source = lax.broadcasted_iota(jnp.int32, (128, 64), 1)
     for n in range(4):
-        first = jnp.broadcast_to(ltab[:, 2 * n : 2 * n + 1], (128, 128))
-        second = jnp.broadcast_to(ltab[:, 2 * n + 1 : 2 * n + 2], (128, 128))
-        table = jnp.where(row // 16 == column // 2, jnp.where(column % 2 == 0, first, second), 0.0)
-        mixn[n] = jnp.dot(onehot, table, preferred_element_type=F32, precision=lax.Precision.HIGHEST)
+        take = jnp.where((column < 16) & (source == (column // 2) * 8 + 2 * n + column % 2), 1.0, 0.0)
+        table = jnp.dot(take, placed, preferred_element_type=F32, precision=exact).T
+        mixn[n] = jnp.dot(onehot, table, preferred_element_type=F32, precision=exact)
     r2[4] = jnp.zeros((CHIPS, 16, TILE), BF)
     r2o[4] = jnp.zeros((CHIPS, 16, TILE), BF)
 
@@ -147,40 +150,52 @@
 
         lax.fori_loop(0, 5, body, 0)
 
-    def second_part(r):
-        rows = pl.ds(r * SPAN, SPAN)
+    def heads_of(r):
         where = pl.ds(pl.multiple_of(opposite * WIDTH, WIDTH), WIDTH)
-        block = full[opposite, rows, :]
-        paired = acc[r % 2, 4] + dot(block, wv[4, where, :])
-        query = unit_rows(paired[:, :DK]).astype(BF)
-        key_t = unit_rows(paired[:, DK:]).T.astype(BF)
-        q[rows, :] = query
-        scores = dot(query, key_t)
+        rows = pl.ds(r * SPAN, SPAN)
+        paired = acc[r % 2, 4] + dot(full[opposite, rows, :], wv[4, where, :])
+        q[rows, :] = unit_rows(paired[:, :DK]).astype(BF)
+        kt[...] = unit_rows(paired[:, DK:]).T.astype(BF)
+
+    def value_of(r, n):
+        where = pl.ds(pl.multiple_of(opposite * WIDTH, WIDTH), WIDTH)
+        rows = pl.ds(r * SPAN, SPAN)
+        return (acc[r % 2, n] + dot(full[opposite, rows, :], wv[n, where, :])).astype(BF)
+
+    def score_of(r):
+        scores = dot(q[pl.ds(r * SPAN, SPAN), :], kt[...])
         t = lax.broadcasted_iota(jnp.int32, (SPAN, SPAN), 0)
         s = lax.broadcasted_iota(jnp.int32, (SPAN, SPAN), 1)
-        scores = jnp.where(t >= s, scores, 0.0).astype(BF)
+        return jnp.where(t >= s, scores, 0.0).astype(BF)
+
+    def near(r, n, scores, value):
+        rows = pl.ds(r * SPAN, SPAN)
+        query = q[rows, :]
+        result = weighted(dot(scores, value), n, rows, 0)
+        if r == 1:
+            result += weighted(dot(query, s0b[n]), n, rows, 1)
+        if r == 3:
+            result += weighted(dot(query, s2b[n]), n, rows, 1)
+        if r >= 2:
+            result += weighted(dot(query, s01[n].astype(BF)), n, rows, 2)
+        mixed[n, rows, :] = result
+
+    def second_part(r):
+        heads_of(r)
+        scores = score_of(r)
 
         def body(n, carry):
-            value = (acc[r % 2, n] + dot(full[opposite, rows, :], wv[n, where, :])).astype(BF)
-            result = weighted(dot(scores, value), n, rows, 0)
-            state = dot(key_t, value)
+            value = value_of(r, n)
+            near(r, n, scores, value)
+            state = dot(kt[...], value)
             if r == 0:
                 s01[n] = state
                 s0b[n] = state.astype(BF)
             elif r == 1:
-                result += weighted(dot(query, s0b[n]), n, rows, 1)
                 s01[n] = s01[n] + state
-            elif r == 2:
-                result += weighted(dot(query, s01[n].astype(BF)), n, rows, 2)
+            else:
                 s2b[n] = state.astype(BF)
                 tot[n] = s01[n] + state
-            else:
-                result += weighted(dot(query, s2b[n]), n, rows, 1)
-                result += weighted(dot(query, s01[n].astype(BF)), n, rows, 2)
-                total = tot[n] + state
-                tot[n] = total
-                tb[n] = total.astype(BF)
-            mixed[n, rows, :] = result
             return carry
 
         lax.fori_loop(0, 4, body, 0)
@@ -199,23 +214,52 @@
             second_part(r - 1)
     for d in range(2):
         forward_in(CHUNKS - 1, d).wait_recv()
-    second_part(CHUNKS - 1)
-
-    core_copy = remote(tb, tpeer, core_sem.at[0], core_sem.at[1], ctx=other)
-    core_copy.start()
-    core_copy.wait_recv()
-    for m in range(2):
-        n = 2 * core + m
-        both = tot[n] + tpeer[n].astype(F32)
-        cb[m * 8 : (m + 1) * 8] = both.astype(BF).reshape(8, 16, TILE)
-
-    def piece(d, carry):
-        dest = lax.rem(chip + d, CHIPS)
-        remote(cb.at[dest], r1.at[chip], one_sem.at[0], one_sem.at[1], ctx=dest * 2 + core).start()
+
+    def core_copy(n):
+        return remote(tb.at[n], tpeer.at[n], core_send.at[n], core_recv.at[n], ctx=other)
+
+    def piece(dest):
+        return remote(cb.at[dest], r1.at[chip], one_sem.at[0], one_sem.at[1], ctx=dest * 2 + core)
+
+    heads_of(3)
+    for order in range(4):
+        n = lax.rem(2 * (1 - core) + order, 4)
+        value = value_of(3, n)
+        last[n] = value
+        total = tot[n] + dot(kt[...], value)
+        tot[n] = total
+        tb[n] = total.astype(BF)
+        core_copy(n).start()
+        if order >= 2:
+            m = order - 2
+            core_copy(n).wait_recv()
+            both = tot[n] + tpeer[n].astype(F32)
+            cb[m * 8 : (m + 1) * 8] = both.astype(BF).reshape(8, 16, TILE)
+
+            def send_piece(d, carry):
+                dest = m * 8 + lax.rem(chip + d, 8)
+
+                @pl.when(dest != chip)
+                def _():
+                    piece(dest).start()
+
+                return carry
+
+            lax.fori_loop(0, 8, send_piece, 0)
+    pair_copy = remote(cb, r2.at[0], pair_sem.at[0], pair_sem.at[1], ctx=lax.rem(ctx + 2, 32))
+
+    @pl.when(bits[0] == 0)
+    def _():
+        pair_copy.start()
+
+    r1[chip] = cb[chip]
+    scores = score_of(3)
+
+    def last_near(n, carry):
+        near(3, n, scores, last[n])
         return carry
 
-    lax.fori_loop(1, CHIPS, piece, 0)
-    r1[chip] = cb[chip]
+    lax.fori_loop(0, 4, last_near, 0)
     others = pl.ds(0, CHIPS - 1)
     remote(cb.at[others], r1.at[others], one_sem.at[0], one_sem.at[1], ctx=other).wait_recv()
 
@@ -226,45 +270,64 @@
     for c in range(CHIPS):
         z, x = c // 4, c % 4
         slot = 0
-        for bit, value in ((x & 1, piece_of[c - 1]), (x & 2, pair[z]), (z & 1, line[z - 1]), (z & 2, lower)):
+        for bit, value in ((x & 2, pair[z]), (z & 1, line[z - 1]), (z & 2, lower)):
             if bit:
-                sb[4 * c + slot] = value.astype(BF)
+                sb[3 * c + slot] = value.astype(BF)
                 slot += 1
 
-    def spread_sums(d, carry):
-        dest = lax.rem(chip + d, CHIPS)
-        dest_count = sum(lax.rem(lax.div(dest, 1 << i), 2) for i in range(4))
-        for j in range(1, 5):
-            @pl.when(dest_count == j)
+    for s in range(1, 4):
+        def send_sum(d, carry):
+            dest = lax.rem(chip + d, CHIPS)
+            dest_count = sum(lax.rem(lax.div(dest, 1 << i), 2) for i in range(1, 4))
+
+            @pl.when(dest_count >= s)
             def _():
                 remote(
-                    sb.at[pl.ds(4 * dest, j)], r2.at[pl.ds(0, j), chip],
-                    two_sem.at[0], two_sem.at[1], ctx=dest * 2 + core,
+                    sb.at[3 * dest + s - 1], r2.at[s, chip],
+                    two_send, two_recv.at[s], ctx=dest * 2 + core,
                 ).start()
-        return carry
-
-    lax.fori_loop(1, CHIPS, spread_sums, 0)
-    for j in range(1, 5):
-        @pl.when(count == j)
+
+            return carry
+
+        lax.fori_loop(1, CHIPS, send_sum, 0)
+
+    for n in range(2):
+        core_copy(2 * (1 - core) + n).wait_recv()
+    core_on = core.astype(F32)
+    for r in range(CHUNKS):
+        def core_level(n, carry):
+            rows = pl.ds(r * SPAN, SPAN)
+            mixed[n, rows, :] = mixed[n, rows, :] + weighted(dot(q[rows, :], tpeer[n]) * core_on, n, rows, 3)
+            return carry
+
+        lax.fori_loop(0, 4, core_level, 0)
+
+    def swap(s):
+        return remote(r2.at[s], r2o.at[s], swap_send.at[s], swap_recv.at[s], ctx=other)
+
+    @pl.when(bits[0] == 1)
+    def _():
+        pair_copy.wait_recv()
+        swap(0).start()
+
+    for s in range(1, 4):
+        @pl.when(count >= s)
         def _():
-            for s in range(j):
-                r2[s, chip] = sb[4 * chip + s]
-            here = r2.at[pl.ds(0, j), pl.ds(0, CHIPS - 1)]
-            remote(here, here, two_sem.at[0], two_sem.at[1], ctx=other).wait_recv()
-            remote(r2.at[pl.ds(0, j)], r2o.at[pl.ds(0, j)], swap_sem.at[0], swap_sem.at[1], ctx=other).start()
-
-    rank = 0
-    slots = []
-    for i in range(4):
+            r2[s, chip] = sb[3 * chip + s - 1]
+            here = r2.at[s, others]
+            remote(here, here, two_send, two_recv.at[s], ctx=other).wait_recv()
+            swap(s).start()
+
+    slots = [4 * (1 - bits[0])]
+    rank = 1
+    for i in range(1, 4):
         slots.append(bits[i] * rank + (1 - bits[i]) * 4)
         rank = rank + bits[i]
-    core_on = core.astype(F32)
 
     def far_tile(r, n, m, source):
         rows = pl.ds(r * SPAN, SPAN)
         query = q[rows, :]
         x = mixed[n, rows, :]
-        x += weighted(dot(query, tpeer[n]) * core_on, n, rows, 3)
         for i in range(4):
             bucket = source[slots[i], pl.ds(pl.multiple_of(m * 8, 8), 8)].reshape(128, TILE)
             x += weighted(dot(query, bucket), n, rows, 4 + i)
@@ -285,11 +348,15 @@
 
         lax.fori_loop(0, 2, near_half, 0)
         if r == 0:
-            for j in range(1, 5):
-                @pl.when(count == j)
+            @pl.when(bits[0] == 1)
+            def _():
+                swap(0).wait_recv()
+
+            for s in range(1, 4):
+                @pl.when(count >= s)
                 def _():
-                    copy = remote(r2.at[pl.ds(0, j)], r2o.at[pl.ds(0, j)], swap_sem.at[0], swap_sem.at[1], ctx=other)
-                    copy.wait_recv()
+                    swap(s).wait_recv()
+
         lax.fori_loop(0, 2, far_half, 0)
 
     def opp_copy(r, d):
@@ -339,13 +406,18 @@
 
         lax.fori_loop(0, 4, body, 0)
 
+    def store(r):
+        rows = pl.ds(r * SPAN, SPAN)
+        return pltpu.make_async_copy(stage.at[rows], out.at[rows], out_sem.at[r])
+
     def finish(r):
         for d in range(2):
             plain_copy(r, d).wait_recv()
             sum_copy(r, d).wait_recv()
         for n in range(4):
             total = pown[r, n].astype(F32) + rpsum[r, 0, n].astype(F32) + rpsum[r, 1, n].astype(F32)
-            out[pl.ds(r * SPAN, SPAN), n * TILE : (n + 1) * TILE] = total.astype(BF)
+            stage[pl.ds(r * SPAN, SPAN), n * TILE : (n + 1) * TILE] = total.astype(BF)
+        store(r).start()
 
     for r in range(CHUNKS):
         far(r)
@@ -357,8 +429,10 @@
             relay(r - 1)
         neighbour_part(r)
         own_part(r)
+        if r > 1:
+            finish(r - 2)
     relay(CHUNKS - 1)
-    for r in range(CHUNKS):
+    for r in range(CHUNKS - 2, CHUNKS):
         finish(r)
 
     for r in range(CHUNKS):
@@ -368,15 +442,27 @@
             opp_copy(r, d).wait_send()
             plain_copy(r, d).wait_send()
             sum_copy(r, d).wait_send()
-    core_copy.wait_send()
+    for r in range(CHUNKS):
+        store(r).wait()
+    for n in range(4):
+        core_copy(n).wait_send()
     remote(cb.at[others], r1.at[others], one_sem.at[0], one_sem.at[1], ctx=other).wait_send()
-    for j in range(0, 5):
+
+    @pl.when(bits[0] == 0)
+    def _():
+        pair_copy.wait_send()
+
+    @pl.when(bits[0] == 1)
+    def _():
+        swap(0).wait_send()
+
+    for j in range(4):
         @pl.when(count == j)
         def _():
-            sent = sb.at[pl.ds(0, 32 - j)]
-            remote(sent, sent, two_sem.at[0], two_sem.at[1], ctx=other).wait_send()
-            if j:
-                remote(r2.at[pl.ds(0, j)], r2o.at[pl.ds(0, j)], swap_sem.at[0], swap_sem.at[1], ctx=other).wait_send()
+            sent = sb.at[pl.ds(0, 24 - j)]
+            remote(sent, sent, two_send, two_recv.at[1], ctx=other).wait_send()
+            for s in range(1, j + 1):
+                swap(s).wait_send()
 
 
 def local(tokens, pair_weight, value_weight, output_weight, level_index, level_table, out_gain):
@@ -388,7 +474,7 @@
         kernel,
         out_shape=jax.ShapeDtypeStruct((rows, WIDTH), BF),
         in_specs=[any_space] * 4 + [vmem] * 3,
-        out_specs=vmem,
+        out_specs=any_space,
         scratch_shapes=[
             pltpu.VMEM((4, rows, WIDTH), BF),
             pltpu.VMEM((5, 4 * WIDTH, TILE), BF),
@@ -396,6 +482,8 @@
             pltpu.VMEM((2, 5, SPAN, TILE), F32),
             pltpu.VMEM((4, rows, 128), F32),
             pltpu.VMEM((rows, DK), BF),
+            pltpu.VMEM((DK, SPAN), BF),
+            pltpu.VMEM((4, SPAN, TILE), BF),
             pltpu.VMEM((4, DK, TILE), F32),
             pltpu.VMEM((4, DK, TILE), BF),
             pltpu.VMEM((4, DK, TILE), BF),
@@ -405,7 +493,7 @@
             pltpu.VMEM((4, rows, TILE), F32),
             pltpu.VMEM((CHIPS, 16, TILE), BF),
             pltpu.VMEM((CHIPS, 16, TILE), BF),
-            pltpu.VMEM((4 * CHIPS, 16, TILE), BF),
+            pltpu.VMEM((3 * CHIPS, 16, TILE), BF),
             pltpu.VMEM((5, CHIPS, 16, TILE), BF),
             pltpu.VMEM((5, CHIPS, 16, TILE), BF),
             pltpu.VMEM((rows, WIDTH), BF),
@@ -414,15 +502,21 @@
             pltpu.VMEM((CHUNKS, 2, 4, SPAN, TILE), BF),
             pltpu.VMEM((CHUNKS, 2, 4, SPAN, TILE), BF),
             pltpu.VMEM((CHUNKS, 4, SPAN, TILE), BF),
+            pltpu.VMEM((rows, WIDTH), BF),
             dma((22,)),
             dma((2, CHUNKS)),
             dma((2, CHUNKS)),
             dma((2, CHUNKS)),
             dma((2, CHUNKS)),
+            dma((4,)),
+            dma((4,)),
             dma((2,)),
             dma((2,)),
-            dma((2,)),
-            dma((2,)),
+            dma(()),
+            dma((4,)),
+            dma((4,)),
+            dma((4,)),
+            dma((CHUNKS,)),
             dma((2, CHUNKS)),
             dma((2, CHUNKS)),
             dma((2, CHUNKS)),
@@ -435,8 +529,8 @@
         ),
         name="layer",
     )(
-        tokens, pair_weight, value_weight, output_weight, level_index,
-        level_table.reshape(128, 8), out_gain.reshape(8, 1, 128),
+        tokens, pair_weight, value_weight, output_weight, level_index.T,
+        level_table.transpose(0, 2, 1).reshape(64, 16), out_gain.reshape(8, 1, 128),
     )
 
 

time: 107 us -> 99.8 us (0.933)
  Pallas kernels: 101 us -> 97.3 us
  local copies, waits for them, and re-layouts: 5.27 us -> 2.26 us
    pallas_call x1, Pallas kernels: 101 us -> 97.3 us  [local(): pl.pallas_call(kernel, out_shape=jax.ShapeDtypeStruct((rows, WIDTH), BF),...]
    unnamed x3 -> x1, local copies, waits for them, and re-layouts: 5.27 us -> 2.26 us
where the time goes in v2:
time: 99.8 us; the launch traced here: 99.6 us
  Pallas kernels  97.3 us (97%)
  local copies, waits for them, and re-layouts  2.26 us (2%)
    pallas_call x1, Pallas kernels, local(): pl.pallas_call(kernel, out_shape=jax.ShapeDtypeStruct((rows, WIDTH), BF),...  97.3 us
    unnamed x1, local copies, waits for them, and re-layouts  2.26 us

profile of v2, /device:TPU:7, one launch (start us, length us, event | category | flops | bytes accessed | tf_op | source)
XLA Modules:
  0.0 99.6 jit_solution(1307908198567708900)
XLA Ops:
  0.0 97.3 %layer.1 = bf16[512,1024]{1,0:T(8,128)(2,1)} custom-call(bf16[512,1024]{1,0:T(8,128)(2,1)} %tok.1, bf16[4096,256]{1,0:T(8,128)(2,1)} %pw.1, bf16[4096,1024]{1,0:T(8,128)(2,1)} %vw.1, bf16[1024,4096]{1,0:T(8,128)(2,1)} %ow.1, s32[8,512]{1,0:T(8,128)} %bitcast.6, f32[64,16]{1,0:T(8,128)} %bitcast.5, f32[8,1,128]{2,1,0:T(1,128)} %bitcast.7), custom_call_target="tpu_custom_call" | custom-call | tf_op jit(solution)/shard_map/layer/pallas_call | solution.py:473
  97.3 2.3 %copy.9 = bf16[512,1024]{1,0:T(8,128)(2,1)} copy(bf16[512,1024]{1,0:T(8,128)(2,1)} %layer.1) | data formatting | bytes 2097152

commit v3 on v2

--- a/solution.py
+++ b/solution.py
@@ -32,9 +32,9 @@
 def kernel(
     tok, pw, vw, ow, lidx, ltab, gain, out,
     full, wv, owv, acc, mixn, q, kt, last, s01, s0b, s2b, tot, tb, tpeer, mixed,
-    cb, r1, sb, r2, r2o, hid, popp, rpopp, psum, rpsum, pown, stage,
+    cb, r1, sb, r2, r2o, hid, popp, rpopp, psum, rpsum, pown,
     w_sem, own_send, own_recv, fwd_send, fwd_recv, core_send, core_recv, one_sem, pair_sem, two_send, two_recv,
-    swap_send, swap_recv, out_sem,
+    swap_send, swap_recv,
     opp_send, opp_recv, plain_send, plain_recv, sum_send, sum_recv,
 ):
     me = lax.axis_index("head")
@@ -47,6 +47,11 @@
     other = ctx + 1 - 2 * core
     bits = [lax.rem(lax.div(chip, 1 << i), 2) for i in range(4)]
     count = bits[1] + bits[2] + bits[3]
+    z_of = [lax.rem(lax.div(chip, 4) + d, 4) for d in range(4)]
+    x_of = [lax.rem(lax.rem(chip, 4) + d, 4) for d in range(4)]
+    z_count = [lax.rem(z, 2) + lax.div(z, 2) for z in z_of]
+    x_count = [lax.div(x, 2) for x in x_of]
+    ring = [(dz, dx) for dz in range(4) for dx in range(4) if dz or dx]
 
     def remote(src, dst, send, recv, **axes):
         return pltpu.make_async_remote_copy(
@@ -70,12 +75,9 @@
         pl.semaphore_signal(barrier, inc=1, device_id={"head": peer}, device_id_type=MESH)
     pl.semaphore_signal(barrier, inc=1, device_id={"ctx": other}, device_id_type=MESH)
 
-    def greet(d, carry):
-        dest = lax.rem(chip + d, CHIPS) * 2 + core
+    for dz, dx in ring:
+        dest = (4 * z_of[dz] + x_of[dx]) * 2 + core
         pl.semaphore_signal(barrier, inc=1, device_id={"ctx": dest}, device_id_type=MESH)
-        return carry
-
-    lax.fori_loop(1, CHIPS, greet, 0)
     tok_load.start()
     for load in loads:
         load.start()
@@ -221,12 +223,18 @@
     def piece(dest):
         return remote(cb.at[dest], r1.at[chip], one_sem.at[0], one_sem.at[1], ctx=dest * 2 + core)
 
-    heads_of(3)
+    end_rows = pl.ds(3 * SPAN, SPAN)
+    end_where = pl.ds(pl.multiple_of(opposite * WIDTH, WIDTH), WIDTH)
+    key = acc[1, 4, :, DK:] + dot(full[opposite, end_rows, :], wv[4, end_where, DK:])
+    values = []
+    for order in range(4):
+        values.append(value_of(3, lax.rem(2 * (1 - core) + order, 4)))
+    key_t = unit_rows(key).T.astype(BF)
+    kt[...] = key_t
     for order in range(4):
         n = lax.rem(2 * (1 - core) + order, 4)
-        value = value_of(3, n)
-        last[n] = value
-        total = tot[n] + dot(kt[...], value)
+        last[n] = values[order]
+        total = tot[n] + dot(key_t, values[order])
         tot[n] = total
         tb[n] = total.astype(BF)
         core_copy(n).start()
@@ -236,16 +244,17 @@
             both = tot[n] + tpeer[n].astype(F32)
             cb[m * 8 : (m + 1) * 8] = both.astype(BF).reshape(8, 16, TILE)
 
-            def send_piece(d, carry):
-                dest = m * 8 + lax.rem(chip + d, 8)
-
-                @pl.when(dest != chip)
-                def _():
-                    piece(dest).start()
-
-                return carry
-
-            lax.fori_loop(0, 8, send_piece, 0)
+            for dz in range(2):
+                z = 2 * m + lax.rem(z_of[0] + dz, 2)
+                for dx in range(4):
+                    dest = 4 * z + x_of[dx]
+                    if dx:
+                        piece(dest).start()
+                    else:
+                        @pl.when(dest != chip)
+                        def _():
+                            piece(dest).start()
+
     pair_copy = remote(cb, r2.at[0], pair_sem.at[0], pair_sem.at[1], ctx=lax.rem(ctx + 2, 32))
 
     @pl.when(bits[0] == 0)
@@ -253,6 +262,8 @@
         pair_copy.start()
 
     r1[chip] = cb[chip]
+    query = acc[1, 4, :, :DK] + dot(full[opposite, end_rows, :], wv[4, end_where, :DK])
+    q[end_rows, :] = unit_rows(query).astype(BF)
     scores = score_of(3)
 
     def last_near(n, carry):
@@ -276,47 +287,32 @@
                 slot += 1
 
     for s in range(1, 4):
-        def send_sum(d, carry):
-            dest = lax.rem(chip + d, CHIPS)
-            dest_count = sum(lax.rem(lax.div(dest, 1 << i), 2) for i in range(1, 4))
-
-            @pl.when(dest_count >= s)
+        for dz, dx in ring:
+            dest = 4 * z_of[dz] + x_of[dx]
+
+            @pl.when(z_count[dz] + x_count[dx] >= s)
             def _():
                 remote(
                     sb.at[3 * dest + s - 1], r2.at[s, chip],
                     two_send, two_recv.at[s], ctx=dest * 2 + core,
                 ).start()
 
-            return carry
-
-        lax.fori_loop(1, CHIPS, send_sum, 0)
 
     for n in range(2):
         core_copy(2 * (1 - core) + n).wait_recv()
     core_on = core.astype(F32)
-    for r in range(CHUNKS):
-        def core_level(n, carry):
-            rows = pl.ds(r * SPAN, SPAN)
+    def core_level(r):
+        rows = pl.ds(r * SPAN, SPAN)
+        def body(n, carry):
             mixed[n, rows, :] = mixed[n, rows, :] + weighted(dot(q[rows, :], tpeer[n]) * core_on, n, rows, 3)
             return carry
 
-        lax.fori_loop(0, 4, core_level, 0)
+        lax.fori_loop(0, 4, body, 0)
+
+    core_level(0)
 
     def swap(s):
         return remote(r2.at[s], r2o.at[s], swap_send.at[s], swap_recv.at[s], ctx=other)
-
-    @pl.when(bits[0] == 1)
-    def _():
-        pair_copy.wait_recv()
-        swap(0).start()
-
-    for s in range(1, 4):
-        @pl.when(count >= s)
-        def _():
-            r2[s, chip] = sb[3 * chip + s - 1]
-            here = r2.at[s, others]
-            remote(here, here, two_send, two_recv.at[s], ctx=other).wait_recv()
-            swap(s).start()
 
     slots = [4 * (1 - bits[0])]
     rank = 1
@@ -324,40 +320,65 @@
         slots.append(bits[i] * rank + (1 - bits[i]) * 4)
         rank = rank + bits[i]
 
-    def far_tile(r, n, m, source):
-        rows = pl.ds(r * SPAN, SPAN)
-        query = q[rows, :]
-        x = mixed[n, rows, :]
-        for i in range(4):
-            bucket = source[slots[i], pl.ds(pl.multiple_of(m * 8, 8), 8)].reshape(128, TILE)
-            x += weighted(dot(query, bucket), n, rows, 4 + i)
+    def far_level(r, n, m, source, i):
+        rows = pl.ds(r * SPAN, SPAN)
+        bucket = source[slots[i], m * 8 : m * 8 + 8].reshape(128, TILE)
+        return weighted(dot(q[rows, :], bucket), n, rows, 4 + i)
+
+    def close(r, n, x):
+        rows = pl.ds(r * SPAN, SPAN)
         for h in range(2):
             one = x[:, h * DH : (h + 1) * DH]
             one = one * lax.rsqrt(jnp.mean(one * one, axis=-1, keepdims=True) + EPS)
             one = one * gain[2 * n + h]
             hid[rows, pl.ds(pl.multiple_of(n * TILE + h * DH, DH), DH)] = one.astype(BF)
 
+    first_rows = pl.ds(0, SPAN)
+    for i in range(4):
+        @pl.when(bits[i] == 1)
+        def _():
+            if i == 0:
+                pair_copy.wait_recv()
+            else:
+                r2[slots[i], chip] = sb[3 * chip + slots[i] - 1]
+                here = r2.at[slots[i], others]
+                remote(here, here, two_send, two_recv.at[slots[i]], ctx=other).wait_recv()
+            swap(slots[i]).start()
+
+        for m in range(2):
+            n = 2 * core + m
+            x = mixed[n, first_rows, :] + far_level(0, n, m, r2, i)
+            if i < 3:
+                mixed[n, first_rows, :] = x
+            else:
+                close(0, n, x)
+    for i in range(4):
+        @pl.when(bits[i] == 1)
+        def _():
+            swap(slots[i]).wait_recv()
+
+        for m in range(2):
+            n = 2 - 2 * core + m
+            x = mixed[n, first_rows, :] + far_level(0, n, m, r2o, i)
+            if i < 3:
+                mixed[n, first_rows, :] = x
+            else:
+                close(0, n, x)
+
     def far(r):
-        def near_half(m, carry):
-            far_tile(r, 2 * core + m, m, r2)
+        core_level(r)
+        rows = pl.ds(r * SPAN, SPAN)
+
+        def body(m, carry):
+            for n, source in ((2 * core + m, r2), (2 - 2 * core + m, r2o)):
+                x = mixed[n, rows, :]
+                for i in range(4):
+                    bucket = source[slots[i], pl.ds(pl.multiple_of(m * 8, 8), 8)].reshape(128, TILE)
+                    x += weighted(dot(q[rows, :], bucket), n, rows, 4 + i)
+                close(r, n, x)
             return carry
 
-        def far_half(m, carry):
-            far_tile(r, 2 - 2 * core + m, m, r2o)
-            return carry
-
-        lax.fori_loop(0, 2, near_half, 0)
-        if r == 0:
-            @pl.when(bits[0] == 1)
-            def _():
-                swap(0).wait_recv()
-
-            for s in range(1, 4):
-                @pl.when(count >= s)
-                def _():
-                    swap(s).wait_recv()
-
-        lax.fori_loop(0, 2, far_half, 0)
+        lax.fori_loop(0, 2, body, 0)
 
     def opp_copy(r, d):
         return remote(popp.at[r, d], rpopp.at[r, d], opp_send.at[d, r], opp_recv.at[d, r], head=peers[d])
@@ -374,12 +395,12 @@
         return dot(hid[pl.ds(r * SPAN, SPAN), :], owv[dest * 4 + n])
 
     def opposite_part(r):
-        def body(n, carry):
-            popp[r, lax.div(n, 2), lax.rem(n, 2)] = project(r, opposite, n).astype(BF)
-            return carry
-
-        lax.fori_loop(0, 4, body, 0)
-        for d in range(2):
+        for d in range(2):
+            def body(m, carry):
+                popp[r, d, m] = project(r, opposite, 2 * d + m).astype(BF)
+                return carry
+
+            lax.fori_loop(0, 2, body, 0)
             opp_copy(r, d).start()
 
     def neighbour_part(r):
@@ -406,32 +427,26 @@
 
         lax.fori_loop(0, 4, body, 0)
 
-    def store(r):
-        rows = pl.ds(r * SPAN, SPAN)
-        return pltpu.make_async_copy(stage.at[rows], out.at[rows], out_sem.at[r])
-
     def finish(r):
         for d in range(2):
             plain_copy(r, d).wait_recv()
             sum_copy(r, d).wait_recv()
         for n in range(4):
             total = pown[r, n].astype(F32) + rpsum[r, 0, n].astype(F32) + rpsum[r, 1, n].astype(F32)
-            stage[pl.ds(r * SPAN, SPAN), n * TILE : (n + 1) * TILE] = total.astype(BF)
-        store(r).start()
+            out[pl.ds(r * SPAN, SPAN), n * TILE : (n + 1) * TILE] = total.astype(BF)
 
     for r in range(CHUNKS):
-        far(r)
+        if r > 0:
+            far(r)
         if r == 0:
             for load in ow_loads:
                 load.wait()
         opposite_part(r)
-        if r > 0:
-            relay(r - 1)
         neighbour_part(r)
         own_part(r)
+        relay(r)
         if r > 1:
             finish(r - 2)
-    relay(CHUNKS - 1)
     for r in range(CHUNKS - 2, CHUNKS):
         finish(r)
 
@@ -442,8 +457,6 @@
             opp_copy(r, d).wait_send()
             plain_copy(r, d).wait_send()
             sum_copy(r, d).wait_send()
-    for r in range(CHUNKS):
-        store(r).wait()
     for n in range(4):
         core_copy(n).wait_send()
     remote(cb.at[others], r1.at[others], one_sem.at[0], one_sem.at[1], ctx=other).wait_send()
@@ -472,9 +485,9 @@
     dma = pltpu.SemaphoreType.DMA
     return pl.pallas_call(
         kernel,
-        out_shape=jax.ShapeDtypeStruct((rows, WIDTH), BF),
+        out_shape=pltpu.VMEM((rows, WIDTH), BF),
         in_specs=[any_space] * 4 + [vmem] * 3,
-        out_specs=any_space,
+        out_specs=vmem,
         scratch_shapes=[
             pltpu.VMEM((4, rows, WIDTH), BF),
             pltpu.VMEM((5, 4 * WIDTH, TILE), BF),
@@ -502,7 +515,6 @@
             pltpu.VMEM((CHUNKS, 2, 4, SPAN, TILE), BF),
             pltpu.VMEM((CHUNKS, 2, 4, SPAN, TILE), BF),
             pltpu.VMEM((CHUNKS, 4, SPAN, TILE), BF),
-            pltpu.VMEM((rows, WIDTH), BF),
             dma((22,)),
             dma((2, CHUNKS)),
             dma((2, CHUNKS)),
@@ -516,7 +528,6 @@
             dma((4,)),
             dma((4,)),
             dma((4,)),
-            dma((CHUNKS,)),
             dma((2, CHUNKS)),
             dma((2, CHUNKS)),
             dma((2, CHUNKS)),

time: 99.8 us -> 96.4 us (0.966); the launches traced: 99.6 us -> 94.9 us
  Pallas kernels: 97.3 us -> 93.9 us
  local copies, waits for them, and re-layouts: 2.26 us -> 0.97 us
    pallas_call x1, Pallas kernels: 97.3 us -> 93.9 us  [local(): pl.pallas_call(kernel, out_shape=pltpu.VMEM((rows, WIDTH), BF), in_specs=...]
    unnamed x1, local copies, waits for them, and re-layouts: 2.26 us -> 0.97 us
where the time goes in v3:
time: 96.4 us; the launch traced here: 94.9 us
  Pallas kernels  93.9 us (97%)
  local copies, waits for them, and re-layouts  0.97 us (1%)
    pallas_call x1, Pallas kernels, local(): pl.pallas_call(kernel, out_shape=pltpu.VMEM((rows, WIDTH), BF), in_specs=...  93.9 us

profile of v3, /device:TPU:7, one launch (start us, length us, event | category | flops | bytes accessed | tf_op | source)
XLA Modules:
  0.0 94.9 jit_solution(4353171942883771925)
XLA Ops:
  0.0 93.9 %layer.1 = bf16[512,1024]{1,0:T(8,128)(2,1)S(1)} custom-call(bf16[512,1024]{1,0:T(8,128)(2,1)} %tok.1, bf16[4096,256]{1,0:T(8,128)(2,1)} %pw.1, bf16[4096,1024]{1,0:T(8,128)(2,1)} %vw.1, bf16[1024,4096]{1,0:T(8,128)(2,1)} %ow.1, s32[8,512]{1,0:T(8,128)} %bitcast.6, f32[64,16]{1,0:T(8,128)} %bitcast.5, f32[8,1,128]{2,1,0:T(1,128)} %bitcast.7), custom_call_target="tpu_custom_call" | custom-call | tf_op jit(solution)/shard_map/layer/pallas_call | solution.py:486
  93.9 1.0 %copy.9 = bf16[512,1024]{1,0:T(8,128)(2,1)} copy(bf16[512,1024]{1,0:T(8,128)(2,1)S(1)} %layer.1) | data formatting | bytes 2097152

commit v4 on v3

--- a/solution.py
+++ b/solution.py
@@ -30,7 +30,8 @@
 
 
 def kernel(
-    tok, pw, vw, ow, lidx, ltab, gain, out,
+    tok, pw, vw, ow, lidx_in, ltab_in, gain_in, out,
+    lidx, ltab, gain,
     full, wv, owv, acc, mixn, q, kt, last, s01, s0b, s2b, tot, tb, tpeer, mixed,
     cb, r1, sb, r2, r2o, hid, popp, rpopp, psum, rpsum, pown,
     w_sem, own_send, own_recv, fwd_send, fwd_recv, core_send, core_recv, one_sem, pair_sem, two_send, two_recv,
@@ -78,6 +79,12 @@
     for dz, dx in ring:
         dest = (4 * z_of[dz] + x_of[dx]) * 2 + core
         pl.semaphore_signal(barrier, inc=1, device_id={"ctx": dest}, device_id_type=MESH)
+    small = [
+        pltpu.make_async_copy(src, dst, w_sem.at[22 + i])
+        for i, (src, dst) in enumerate(((lidx_in, lidx), (ltab_in, ltab), (gain_in, gain)))
+    ]
+    for load in small:
+        load.start()
     tok_load.start()
     for load in loads:
         load.start()
@@ -108,6 +115,8 @@
         for d in range(2):
             own(r, d).start()
 
+    for load in small:
+        load.wait()
     row = lax.broadcasted_iota(jnp.int32, (128, 8), 0)
     spread = jnp.where(row // 16 == lax.broadcasted_iota(jnp.int32, (128, 8), 1), 1.0, 0.0).astype(BF)
     wanted = dot(spread, lidx[...].astype(F32).astype(BF))
@@ -262,15 +271,6 @@
         pair_copy.start()
 
     r1[chip] = cb[chip]
-    query = acc[1, 4, :, :DK] + dot(full[opposite, end_rows, :], wv[4, end_where, :DK])
-    q[end_rows, :] = unit_rows(query).astype(BF)
-    scores = score_of(3)
-
-    def last_near(n, carry):
-        near(3, n, scores, last[n])
-        return carry
-
-    lax.fori_loop(0, 4, last_near, 0)
     others = pl.ds(0, CHIPS - 1)
     remote(cb.at[others], r1.at[others], one_sem.at[0], one_sem.at[1], ctx=other).wait_recv()
 
@@ -286,18 +286,39 @@
                 sb[3 * c + slot] = value.astype(BF)
                 slot += 1
 
+    def send_sum(dest, s):
+        remote(
+            sb.at[3 * dest + s - 1], r2.at[s, chip], two_send, two_recv.at[s], ctx=dest * 2 + core
+        ).start()
+
+    for dest in (2, 3):
+        @pl.when(chip != dest)
+        def _():
+            send_sum(dest, 1)
+
+    for s in (1, 2):
+        for dx in range(4):
+            dest = 4 + x_of[dx]
+
+            @pl.when((x_count[dx] >= s - 1) & (chip != dest))
+            def _():
+                send_sum(dest, s)
+
     for s in range(1, 4):
         for dz, dx in ring:
-            dest = 4 * z_of[dz] + x_of[dx]
-
-            @pl.when(z_count[dz] + x_count[dx] >= s)
+            @pl.when((z_count[dz] + x_count[dx] >= s) & (z_of[dz] > 1))
             def _():
-                remote(
-                    sb.at[3 * dest + s - 1], r2.at[s, chip],
-                    two_send, two_recv.at[s], ctx=dest * 2 + core,
-                ).start()
-
-
+                send_sum(4 * z_of[dz] + x_of[dx], s)
+
+    query = acc[1, 4, :, :DK] + dot(full[opposite, end_rows, :], wv[4, end_where, :DK])
+    q[end_rows, :] = unit_rows(query).astype(BF)
+    scores = score_of(3)
+
+    def last_near(n, carry):
+        near(3, n, scores, last[n])
+        return carry
+
+    lax.fori_loop(0, 4, last_near, 0)
     for n in range(2):
         core_copy(2 * (1 - core) + n).wait_recv()
     core_on = core.astype(F32)
@@ -486,9 +507,12 @@
     return pl.pallas_call(
         kernel,
         out_shape=pltpu.VMEM((rows, WIDTH), BF),
-        in_specs=[any_space] * 4 + [vmem] * 3,
+        in_specs=[any_space] * 7,
         out_specs=vmem,
         scratch_shapes=[
+            pltpu.VMEM((8, rows), jnp.int32),
+            pltpu.VMEM((64, 16), F32),
+            pltpu.VMEM((8, 1, DH), F32),
             pltpu.VMEM((4, rows, WIDTH), BF),
             pltpu.VMEM((5, 4 * WIDTH, TILE), BF),
             pltpu.VMEM((16, WIDTH, TILE), BF),
@@ -515,7 +539,7 @@
             pltpu.VMEM((CHUNKS, 2, 4, SPAN, TILE), BF),
             pltpu.VMEM((CHUNKS, 2, 4, SPAN, TILE), BF),
             pltpu.VMEM((CHUNKS, 4, SPAN, TILE), BF),
-            dma((22,)),
+            dma((25,)),
             dma((2, CHUNKS)),
             dma((2, CHUNKS)),
             dma((2, CHUNKS)),

time: 96.4 us -> 95.2 us (0.988)
  Pallas kernels: 93.9 us -> 92.5 us
    pallas_call x1, Pallas kernels: 93.9 us -> 92.5 us  [local(): pl.pallas_call(kernel, out_shape=pltpu.VMEM((rows, WIDTH), BF), in_specs=...]
where the time goes in v4:
time: 95.2 us; the launch traced here: 93.4 us
  Pallas kernels  92.5 us (97%)
  local copies, waits for them, and re-layouts  0.97 us (1%)
    pallas_call x1, Pallas kernels, local(): pl.pallas_call(kernel, out_shape=pltpu.VMEM((rows, WIDTH), BF), in_specs=...  92.5 us

profile of v4, /device:TPU:7, one launch (start us, length us, event | category | flops | bytes accessed | tf_op | source)
XLA Modules:
  0.0 93.4 jit_solution(11004331326411967151)
XLA Ops:
  0.0 92.5 %layer.1 = bf16[512,1024]{1,0:T(8,128)(2,1)S(1)} custom-call(bf16[512,1024]{1,0:T(8,128)(2,1)} %tok.1, bf16[4096,256]{1,0:T(8,128)(2,1)} %pw.1, bf16[4096,1024]{1,0:T(8,128)(2,1)} %vw.1, bf16[1024,4096]{1,0:T(8,128)(2,1)} %ow.1, s32[8,512]{1,0:T(8,128)} %bitcast.6, f32[64,16]{1,0:T(8,128)} %bitcast.5, f32[8,1,128]{2,1,0:T(1,128)} %bitcast.7), custom_call_target="tpu_custom_call" | custom-call | tf_op jit(solution)/shard_map/layer/pallas_call | solution.py:507
  92.5 1.0 %copy.9 = bf16[512,1024]{1,0:T(8,128)(2,1)} copy(bf16[512,1024]{1,0:T(8,128)(2,1)S(1)} %layer.1) | data formatting | bytes 2097152

commit v5 on v4

--- a/solution.py
+++ b/solution.py
@@ -416,13 +416,12 @@
         return dot(hid[pl.ds(r * SPAN, SPAN), :], owv[dest * 4 + n])
 
     def opposite_part(r):
-        for d in range(2):
-            def body(m, carry):
+        for m in range(2):
+            for d in range(2):
                 popp[r, d, m] = project(r, opposite, 2 * d + m).astype(BF)
-                return carry
-
-            lax.fori_loop(0, 2, body, 0)
-            opp_copy(r, d).start()
+                remote(
+                    popp.at[r, d, m], rpopp.at[r, d, m], opp_send.at[d, r], opp_recv.at[d, r], head=peers[d]
+                ).start()
 
     def neighbour_part(r):
         for d in range(2):
@@ -456,15 +455,14 @@
             total = pown[r, n].astype(F32) + rpsum[r, 0, n].astype(F32) + rpsum[r, 1, n].astype(F32)
             out[pl.ds(r * SPAN, SPAN), n * TILE : (n + 1) * TILE] = total.astype(BF)
 
+    for load in ow_loads:
+        load.wait()
     for r in range(CHUNKS):
-        if r > 0:
-            far(r)
-        if r == 0:
-            for load in ow_loads:
-                load.wait()
         opposite_part(r)
         neighbour_part(r)
         own_part(r)
+        if r + 1 < CHUNKS:
+            far(r + 1)
         relay(r)
         if r > 1:
             finish(r - 2)

time: 95.2 us -> 94.7 us (level)
  no operation moved by 1% of the time
where the time goes in v5:
time: 94.7 us; the launch traced here: 93.7 us
  Pallas kernels  92.7 us (98%)
  local copies, waits for them, and re-layouts  0.97 us (1%)
    pallas_call x1, Pallas kernels, local(): pl.pallas_call(kernel, out_shape=pltpu.VMEM((rows, WIDTH), BF), in_specs=...  92.7 us

profile of v5, /device:TPU:7, one launch (start us, length us, event | category | flops | bytes accessed | tf_op | source)
XLA Modules:
  0.0 93.7 jit_solution(12665275347425117167)
XLA Ops:
  0.0 92.7 %layer.1 = bf16[512,1024]{1,0:T(8,128)(2,1)S(1)} custom-call(bf16[512,1024]{1,0:T(8,128)(2,1)} %tok.1, bf16[4096,256]{1,0:T(8,128)(2,1)} %pw.1, bf16[4096,1024]{1,0:T(8,128)(2,1)} %vw.1, bf16[1024,4096]{1,0:T(8,128)(2,1)} %ow.1, s32[8,512]{1,0:T(8,128)} %bitcast.6, f32[64,16]{1,0:T(8,128)} %bitcast.5, f32[8,1,128]{2,1,0:T(1,128)} %bitcast.7), custom_call_target="tpu_custom_call" | custom-call | tf_op jit(solution)/shard_map/layer/pallas_call | solution.py:505
  92.7 1.0 %copy.9 = bf16[512,1024]{1,0:T(8,128)(2,1)} copy(bf16[512,1024]{1,0:T(8,128)(2,1)S(1)} %layer.1) | data formatting | bytes 2097152

commit v6 on v5

--- a/solution.py
+++ b/solution.py
@@ -76,7 +76,7 @@
         pl.semaphore_signal(barrier, inc=1, device_id={"head": peer}, device_id_type=MESH)
     pl.semaphore_signal(barrier, inc=1, device_id={"ctx": other}, device_id_type=MESH)
 
-    for dz, dx in ring:
+    for dz, dx in sorted(ring, key=lambda step: (2, 1, 3, 0).index(step[0])):
         dest = (4 * z_of[dz] + x_of[dx]) * 2 + core
         pl.semaphore_signal(barrier, inc=1, device_id={"ctx": dest}, device_id_type=MESH)
     small = [
@@ -310,15 +310,6 @@
             def _():
                 send_sum(4 * z_of[dz] + x_of[dx], s)
 
-    query = acc[1, 4, :, :DK] + dot(full[opposite, end_rows, :], wv[4, end_where, :DK])
-    q[end_rows, :] = unit_rows(query).astype(BF)
-    scores = score_of(3)
-
-    def last_near(n, carry):
-        near(3, n, scores, last[n])
-        return carry
-
-    lax.fori_loop(0, 4, last_near, 0)
     for n in range(2):
         core_copy(2 * (1 - core) + n).wait_recv()
     core_on = core.astype(F32)
@@ -355,7 +346,14 @@
             hid[rows, pl.ds(pl.multiple_of(n * TILE + h * DH, DH), DH)] = one.astype(BF)
 
     first_rows = pl.ds(0, SPAN)
-    for i in range(4):
+    for load in ow_loads:
+        load.wait()
+
+    def half_share(n, half):
+        depth = pl.ds(pl.multiple_of(half * (WIDTH // 2), WIDTH // 2), WIDTH // 2)
+        return dot(hid[first_rows, depth], owv[opposite * 4 + n, depth, :])
+
+    def own_level(i):
         @pl.when(bits[i] == 1)
         def _():
             if i == 0:
@@ -365,27 +363,28 @@
                 here = r2.at[slots[i], others]
                 remote(here, here, two_send, two_recv.at[slots[i]], ctx=other).wait_recv()
             swap(slots[i]).start()
-
-        for m in range(2):
-            n = 2 * core + m
-            x = mixed[n, first_rows, :] + far_level(0, n, m, r2, i)
-            if i < 3:
-                mixed[n, first_rows, :] = x
-            else:
-                close(0, n, x)
-    for i in range(4):
+            for m in range(2):
+                n = 2 * core + m
+                mixed[n, first_rows, :] = mixed[n, first_rows, :] + far_level(0, n, m, r2, i)
+
+    def other_level(i):
         @pl.when(bits[i] == 1)
         def _():
             swap(slots[i]).wait_recv()
-
-        for m in range(2):
-            n = 2 - 2 * core + m
-            x = mixed[n, first_rows, :] + far_level(0, n, m, r2o, i)
-            if i < 3:
-                mixed[n, first_rows, :] = x
-            else:
-                close(0, n, x)
-
+            for m in range(2):
+                n = 2 - 2 * core + m
+                mixed[n, first_rows, :] = mixed[n, first_rows, :] + far_level(0, n, m, r2o, i)
+
+    for i in range(4):
+        own_level(i)
+    for m in range(2):
+        close(0, 2 * core + m, mixed[2 * core + m, first_rows, :])
+    for n in range(4):
+        acc[0, n] = half_share(n, core)
+    for i in range(4):
+        other_level(i)
+    for m in range(2):
+        close(0, 2 - 2 * core + m, mixed[2 - 2 * core + m, first_rows, :])
     def far(r):
         core_level(r)
         rows = pl.ds(r * SPAN, SPAN)
@@ -401,6 +400,17 @@
 
         lax.fori_loop(0, 2, body, 0)
 
+    def end_near():
+        query = acc[1, 4, :, :DK] + dot(full[opposite, end_rows, :], wv[4, end_where, :DK])
+        q[end_rows, :] = unit_rows(query).astype(BF)
+        scores = score_of(3)
+
+        def last_near(n, carry):
+            near(3, n, scores, last[n])
+            return carry
+
+        lax.fori_loop(0, 4, last_near, 0)
+
     def opp_copy(r, d):
         return remote(popp.at[r, d], rpopp.at[r, d], opp_send.at[d, r], opp_recv.at[d, r], head=peers[d])
 
@@ -418,7 +428,9 @@
     def opposite_part(r):
         for m in range(2):
             for d in range(2):
-                popp[r, d, m] = project(r, opposite, 2 * d + m).astype(BF)
+                n = 2 * d + m
+                share = acc[0, n] + half_share(n, 1 - core) if r == 0 else project(r, opposite, n)
+                popp[r, d, m] = share.astype(BF)
                 remote(
                     popp.at[r, d, m], rpopp.at[r, d, m], opp_send.at[d, r], opp_recv.at[d, r], head=peers[d]
                 ).start()
@@ -455,19 +467,20 @@
             total = pown[r, n].astype(F32) + rpsum[r, 0, n].astype(F32) + rpsum[r, 1, n].astype(F32)
             out[pl.ds(r * SPAN, SPAN), n * TILE : (n + 1) * TILE] = total.astype(BF)
 
-    for load in ow_loads:
-        load.wait()
     for r in range(CHUNKS):
         opposite_part(r)
         neighbour_part(r)
-        own_part(r)
+        if r > 0:
+            own_part(r - 1)
+        if r == 1:
+            end_near()
         if r + 1 < CHUNKS:
             far(r + 1)
         relay(r)
         if r > 1:
             finish(r - 2)
-    for r in range(CHUNKS - 2, CHUNKS):
-        finish(r)
+    own_part(CHUNKS - 1)
+    finish(CHUNKS - 2)
 
     for r in range(CHUNKS):
         for d in range(2):
@@ -475,7 +488,8 @@
             forward(r, d).wait_send()
             opp_copy(r, d).wait_send()
             plain_copy(r, d).wait_send()
-            sum_copy(r, d).wait_send()
+            if r < CHUNKS - 1:
+                sum_copy(r, d).wait_send()
     for n in range(4):
         core_copy(n).wait_send()
     remote(cb.at[others], r1.at[others], one_sem.at[0], one_sem.at[1], ctx=other).wait_send()
@@ -495,6 +509,10 @@
             remote(sent, sent, two_send, two_recv.at[1], ctx=other).wait_send()
             for s in range(1, j + 1):
                 swap(s).wait_send()
+
+    finish(CHUNKS - 1)
+    for d in range(2):
+        sum_copy(CHUNKS - 1, d).wait_send()
 
 
 def local(tokens, pair_weight, value_weight, output_weight, level_index, level_table, out_gain):

time: 94.7 us -> 94.4 us (level)
  no operation moved by 1% of the time
where the time goes in v6:
time: 94.4 us; the launch traced here: 93.5 us
  Pallas kernels  92.5 us (98%)
  local copies, waits for them, and re-layouts  0.97 us (1%)
    pallas_call x1, Pallas kernels, local(): pl.pallas_call(kernel, out_shape=pltpu.VMEM((rows, WIDTH), BF), in_specs=...  92.5 us

profile of v6, /device:TPU:7, one launch (start us, length us, event | category | flops | bytes accessed | tf_op | source)
XLA Modules:
  0.0 93.5 jit_solution(4199830686316101518)
XLA Ops:
  0.0 92.5 %layer.1 = bf16[512,1024]{1,0:T(8,128)(2,1)S(1)} custom-call(bf16[512,1024]{1,0:T(8,128)(2,1)} %tok.1, bf16[4096,256]{1,0:T(8,128)(2,1)} %pw.1, bf16[4096,1024]{1,0:T(8,128)(2,1)} %vw.1, bf16[1024,4096]{1,0:T(8,128)(2,1)} %ow.1, s32[8,512]{1,0:T(8,128)} %bitcast.6, f32[64,16]{1,0:T(8,128)} %bitcast.5, f32[8,1,128]{2,1,0:T(1,128)} %bitcast.7), custom_call_target="tpu_custom_call" | custom-call | tf_op jit(solution)/shard_map/layer/pallas_call | solution.py:523
  92.5 1.0 %copy.9 = bf16[512,1024]{1,0:T(8,128)(2,1)} copy(bf16[512,1024]{1,0:T(8,128)(2,1)S(1)} %layer.1) | data formatting | bytes 2097152

commit v7 on v6

--- a/solution.py
+++ b/solution.py
@@ -450,7 +450,9 @@
             for m in range(2):
                 n = 2 * d + m
                 psum[r, d, n] = (psum[r, d, n].astype(F32) + rpopp[r, d, m].astype(F32)).astype(BF)
-            sum_copy(r, d).start()
+                remote(
+                    psum.at[r, d, n], rpsum.at[r, d, n], sum_send.at[d, r], sum_recv.at[d, r], head=peers[d]
+                ).start()
 
     def own_part(r):
         def body(n, carry):

time: 94.4 us -> 94.5 us (level)
  no operation moved by 1% of the time
where the time goes in v7:
time: 94.5 us; the launch traced here: 93.5 us
  Pallas kernels  92.5 us (98%)
  local copies, waits for them, and re-layouts  0.97 us (1%)
    pallas_call x1, Pallas kernels, local(): pl.pallas_call(kernel, out_shape=pltpu.VMEM((rows, WIDTH), BF), in_specs=...  92.5 us

profile of v7, /device:TPU:7, one launch (start us, length us, event | category | flops | bytes accessed | tf_op | source)
XLA Modules:
  0.0 93.5 jit_solution(7621830122055223405)
XLA Ops:
  0.0 92.5 %layer.1 = bf16[512,1024]{1,0:T(8,128)(2,1)S(1)} custom-call(bf16[512,1024]{1,0:T(8,128)(2,1)} %tok.1, bf16[4096,256]{1,0:T(8,128)(2,1)} %pw.1, bf16[4096,1024]{1,0:T(8,128)(2,1)} %vw.1, bf16[1024,4096]{1,0:T(8,128)(2,1)} %ow.1, s32[8,512]{1,0:T(8,128)} %bitcast.6, f32[64,16]{1,0:T(8,128)} %bitcast.5, f32[8,1,128]{2,1,0:T(1,128)} %bitcast.7), custom_call_target="tpu_custom_call" | custom-call | tf_op jit(solution)/shard_map/layer/pallas_call | solution.py:525
  92.6 1.0 %copy.9 = bf16[512,1024]{1,0:T(8,128)(2,1)} copy(bf16[512,1024]{1,0:T(8,128)(2,1)S(1)} %layer.1) | data formatting | bytes 2097152
